TPU v7x, 32 devices: a whole 2x2x4 slice. The times are simulated.
32 devices in a mesh: ga: 2 (over y), aa: 4 (over x, core), ba: 4 (over z).
Axes of the slice: x: 2, y: 2, z: 4, core: 2. Of those that a mesh axis runs over, the one named last changes fastest.
Arguments:
- query: bfloat16 [2048, 5120], P(('ga', 'aa'), 'ba'), parts along dimension 0, may hold values from -64 to 64
- keys: bfloat16 [16384, 1024], P(('ga', 'aa'), 'ba'), parts along dimension 0, may hold values from -16 to 16
- values: bfloat16 [16384, 1024], P(('ga', 'aa'), 'ba'), parts along dimension 0, may hold values from -6 to 6
- cache_lengths: int32 [8], P(('ga', 'aa')), parts along dimension 0, may hold values from 256 to 2048, as said below
- residual: bfloat16 [2048, 5120], P(('ga', 'ba'), 'aa'), parts along dimension 0, may hold values from -16 to 16
- out_weight: bfloat16 [5120, 5120], P('ba', 'aa'), may hold values from -0.078125 to 0.078125
- norm_gain: float32 [5120], P('aa'), may hold values from 0.1 to 1.9
- router_weight: float32 [5120, 4], P('aa'), may hold values from -0.078125 to 0.078125
- expert_ids: int32 [2048], P(('ga', 'ba')), parts along dimension 0, may hold values from 0 to 3
- expert_slots: int32 [2048], P(('ga', 'ba')), parts along dimension 0, may hold values from -1 to 127, as said below
- expert_gate: bfloat16 [4, 5120, 4096], P('ba', None, 'aa'), may hold values from -0.078125 to 0.078125
- expert_up: bfloat16 [4, 5120, 4096], P('ba', None, 'aa'), may hold values from -0.078125 to 0.078125
- expert_down: bfloat16 [4, 4096, 5120], P('ba', 'aa'), may hold values from -0.25 to 0.25
Outputs:
- layer_out: bfloat16 [2048, 5120], P(('ga', 'ba'), 'aa'), parts along dimension 0
There are 2 independent parts, one for each index of `ga`. A program takes and returns all parts, laid end to end along the dimension named above; an argument that names none is the same for every part. Nothing has to cross between parts.
Inputs may be any that keep to these rules, and one draw needn't show every extreme that they name: `cache_lengths`: some shard has 2048 valid positions in every draw. `expert_slots`: rows form aligned blocks of 256 rows (the rows of one index of ba). A row's slot is the number of earlier rows of its block with the same expert id, or -1 where that number is 128 or more. In every draw some expert has all 128 slots filled in every block.
All inputs are finite; a program needn't handle non-finite values.
Results may differ from a plain program's by a relative error of at most 0.019.
Values may be sent and summed in bfloat16 or wider, within the bound.
A program may use at most 128 MiB of HBM per device.

v0:
```python
import jax
import jax.numpy as jnp
from jax import lax
from jax.sharding import PartitionSpec as P

D = 5120
HD = 128
Q = 1024
CTX_DEV = 2048


NEGATIVE = -1e30
EPSILON = 1e-05


def head_partials(rows, key_block, value_block, length):
    heads = rows.shape[1] // HD
    kv_heads = key_block.shape[1] // HD
    group = heads // kv_heads
    valid = lax.broadcasted_iota(jnp.int32, (1, key_block.shape[0]), 1) < length
    maxima = []
    totals = []
    outputs = []
    for head in range(heads):
        source = head // group
        q_head = rows[:, head * HD : (head + 1) * HD]
        k_head = key_block[:, source * HD : (source + 1) * HD]
        v_head = value_block[:, source * HD : (source + 1) * HD]
        scores = lax.dot_general(
            q_head, k_head, (((1,), (1,)), ((), ())), preferred_element_type=jnp.float32
        ) * HD ** (-0.5)
        scores = jnp.where(valid, scores, NEGATIVE)
        peak = jnp.max(scores, axis=1)
        probs = jnp.exp(scores - peak[:, None])
        maxima.append(peak)
        totals.append(jnp.sum(probs, axis=1))
        outputs.append(
            jnp.dot(probs.astype(jnp.bfloat16), v_head, preferred_element_type=jnp.float32)
        )
    return (jnp.stack(maxima, axis=1), jnp.stack(totals, axis=1), jnp.concatenate(outputs, axis=1))


def combine_partials(first, second):
    peak_one, total_one, out_one = first
    peak_two, total_two, out_two = second
    peak = jnp.maximum(peak_one, peak_two)
    scale_one = jnp.exp(peak_one - peak)
    scale_two = jnp.exp(peak_two - peak)
    outputs = out_one * jnp.repeat(scale_one, HD, axis=1) + out_two * jnp.repeat(
        scale_two, HD, axis=1
    )
    return (peak, total_one * scale_one + total_two * scale_two, outputs)


def on_device(
    query,
    keys,
    values,
    cache_lengths,
    residual,
    out_weight,
    norm_gain,
    router_weight,
    expert_ids,
    expert_slots,
    expert_gate,
    expert_up,
    expert_down,
):
    heads = query.shape[1] // HD
    own_rows = query.shape[0]
    start_state = (
        jnp.full((own_rows, heads), NEGATIVE, jnp.float32),
        jnp.zeros((own_rows, heads), jnp.float32),
        jnp.zeros((own_rows, heads * HD), jnp.float32),
    )
    key_piece = lax.all_gather(keys, "aa", axis=0, tiled=True)
    value_piece = lax.all_gather(values, "aa", axis=0, tiled=True)
    length_piece = lax.all_gather(cache_lengths, "aa", axis=0, tiled=True)

    def one_shard(index, carry):
        key_block = lax.dynamic_slice_in_dim(key_piece, index * CTX_DEV, CTX_DEV, 0)
        value_block = lax.dynamic_slice_in_dim(value_piece, index * CTX_DEV, CTX_DEV, 0)
        return combine_partials(
            carry, head_partials(query, key_block, value_block, length_piece[index])
        )

    peak, total, weighted = lax.fori_loop(0, length_piece.shape[0], one_shard, start_state)
    own = (weighted / jnp.repeat(total, HD, axis=1)).astype(jnp.bfloat16)
    attended = lax.all_gather(own, "aa", axis=0, tiled=True)
    hidden = residual.astype(jnp.float32) + lax.psum_scatter(
        jnp.dot(attended, out_weight, preferred_element_type=jnp.float32).astype(jnp.bfloat16),
        "ba",
        scatter_dimension=0,
        tiled=True,
    ).astype(jnp.float32)
    squares = lax.psum(jnp.sum(hidden * hidden, axis=1), "aa")
    inverse = 1.0 / jnp.sqrt(squares / D + EPSILON)
    normed = hidden * inverse[:, None] * norm_gain
    logits = lax.psum(jnp.dot(normed, router_weight, precision=lax.Precision.HIGHEST), "aa")
    experts = router_weight.shape[1]
    chosen = expert_ids[:, None] == lax.broadcasted_iota(jnp.int32, (1, experts), 1)
    gate = jnp.sum(jnp.where(chosen, jax.nn.sigmoid(logits), 0.0), axis=1)
    expert_in = normed.astype(jnp.bfloat16)
    slot_count = 2 * Q // (lax.axis_size("ba") * experts)
    combined = expert_ids * slot_count + expert_slots
    placing = (
        combined[:, None] == lax.broadcasted_iota(jnp.int32, (1, experts * slot_count), 1)
    ) & (expert_slots[:, None] >= 0)
    placing = placing.astype(jnp.bfloat16)
    packed = lax.dot_general(
        placing, expert_in, (((0,), (0,)), ((), ())), preferred_element_type=jnp.float32
    ).astype(jnp.bfloat16)
    arrived = lax.all_to_all(packed, "ba", split_axis=0, concat_axis=0, tiled=True)
    gate_w = expert_gate[0]
    up_w = expert_up[0]
    down_w = expert_down[0]
    piece = lax.all_gather(arrived, "aa", axis=1, tiled=True)
    gate_part = jnp.dot(piece, gate_w, preferred_element_type=jnp.float32)
    up_part = jnp.dot(piece, up_w, preferred_element_type=jnp.float32)
    act = (jax.nn.silu(gate_part) * up_part).astype(jnp.bfloat16)
    expert_out = lax.psum_scatter(
        lax.dot_general(
            down_w, act, (((0,), (1,)), ((), ())), preferred_element_type=jnp.float32
        ).astype(jnp.bfloat16),
        "aa",
        scatter_dimension=0,
        tiled=True,
    )
    returned = lax.all_to_all(expert_out, "ba", split_axis=1, concat_axis=1, tiled=True)
    from_experts = lax.dot_general(
        placing, returned, (((1,), (1,)), ((), ())), preferred_element_type=jnp.float32
    )
    return (hidden + gate[:, None] * from_experts).astype(jnp.bfloat16)


def solution(mesh):
    return jax.shard_map(
        on_device,
        mesh=mesh,
        in_specs=(
            P(("ga", "aa"), "ba"),
            P(("ga", "aa"), "ba"),
            P(("ga", "aa"), "ba"),
            P(("ga", "aa")),
            P(("ga", "ba"), "aa"),
            P("ba", "aa"),
            P("aa"),
            P("aa", None),
            P(("ga", "ba")),
            P(("ga", "ba")),
            P("ba", None, "aa"),
            P("ba", None, "aa"),
            P("ba", "aa", None),
        ),
        out_specs=P(("ga", "ba"), "aa"),
        check_vma=False,
    )
```

profile of v0, /device:TPU:0, one launch (start us, length us, event | category | flops | bytes accessed | tf_op | source)
XLA Modules:
  0.0 473.7 jit_solution(9405329389665705424)
XLA Ops:
  6.5 0.7 all-gather.5.cloned.1.call-update
  7.3 0.7 all-gather.7.cloned.1.call-update
  8.7 0.6 dynamic-slice
  9.3 0.8 dynamic-update-slice
  10.1 6.4 %all-reduce = s32[4]{0:T(128)S(1)} all-reduce(s32[4]{0:T(128)S(1)} %dynamic-update-slice), channel_id=1, replica_groups=mesh['ga'=2,'aa'=4,'ba'=4] {'aa'}, use_global_device_ids=true, to_apply=%add | all-reduce | flops 4 | bytes 32
  16.4 29.7 %all-gather.5.cloned.1.call-done = bf16[8192,256]{1,0:T(8,128)(2,1)} async-done(((bf16[2048,256]{1,0:T(8,128)(2,1)}), bf16[8192,256]{1,0:T(8,128)(2,1)}) %all-gather.5.cloned.1.call-update) | async-done | bytes 4194320 | tf_op jit(solution)/shard_map/all_gather | solution.py:77
  46.1 36.0 %all-gather.7.cloned.1.call-done = bf16[8192,256]{1,0:T(8,128)(2,1)} async-done(((bf16[2048,256]{1,0:T(8,128)(2,1)}), bf16[8192,256]{1,0:T(8,128)(2,1)}) %all-gather.7.cloned.1.call-update) | async-done | bytes 4194320 | tf_op jit(solution)/shard_map/all_gather | solution.py:78
  82.2 92.8 %while.18 = (s32[]{:T(128)}, f32[256,10]{0,1:T(8,128)S(1)}, f32[256,10]{0,1:T(8,128)S(1)}, f32[256,1280]{0,1:T(8,128)}, s32[4]{0:T(128)S(1)}, /*index=5*/bf16[81...) while((s32[]{:T(128)}, f32[256,10]{0,1:T(8,128)S(1)}, ...), condition=%wide.region_21.22_spmd.clone, body=%wide.region_0.21_spmd.clone.sunk | while | flops 2722382848 | bytes 120924600 | solution.py:88
  82.7 0.6 iota_compare_fusion.4
  83.3 1.8 fusion.224
  85.7 1.5 fusion.222
  87.5 0.6 fusion.220
  88.5 0.6 fusion.218
  93.1 0.6 fusion.208
  95.0 1.3 copy-done.3
  101.2 1.2 copy-done.4
  102.5 2.6 fusion.227
  105.6 0.6 iota_compare_fusion.4
  106.2 1.8 fusion.224
  108.6 1.5 fusion.222
  110.4 0.6 fusion.220
  112.3 0.6 fusion.216
  117.9 1.3 copy-done.3
  124.1 1.2 copy-done.4
  125.4 3.0 fusion.227
  128.9 0.6 iota_compare_fusion.4
  129.5 1.8 fusion.224
  131.9 1.5 fusion.222
  133.7 0.6 fusion.220
  134.7 0.6 fusion.218
  135.6 0.6 fusion.216
  137.5 0.6 fusion.212
  138.4 0.6 fusion.210
  139.3 0.6 fusion.208
  140.3 0.6 fusion.206
  141.2 1.3 copy-done.3
  147.4 1.2 copy-done.4
  148.7 3.0 fusion.227
  152.2 0.6 iota_compare_fusion.4
  152.8 1.8 fusion.224
  155.2 1.5 fusion.222
  157.0 0.6 fusion.220
  158.9 0.6 fusion.216
  164.5 1.3 copy-done.3
  170.7 1.2 copy-done.4
  172.0 3.0 fusion.227
  175.0 2.3 fusion.110
  177.3 26.0 %all-gather.9.cloned.1.call-done = bf16[1024,1280]{0,1:T(8,128)(2,1)} async-done(((bf16[256,1280]{0,1:T(8,128)(2,1)}), bf16[1024,1280]{0,1:T(8,128)(2,1)}) %all-gather.9.cloned.1.call-update) | async-done | bytes 2621456 | tf_op jit(solution)/shard_map/all_gather | solution.py:90
  203.3 6.9 %convolution_convert_fusion = bf16[1024,1280]{1,0:T(8,128)(2,1)} fusion(bf16[1024,1280]{0,1:T(8,128)(2,1)} %all-gather.9.cloned.1.call-done, bf16[1280,1280]{1,0:T(8,128)(2,1)S(1)} %copy-done), kind=kOutput, calls=%fused_computation.127 | convolution fusion | flops 3356753920 | bytes 8519680 | tf_op jit(solution)/shard_map/dot_general | solution.py:92
  210.2 0.6 copy-done.8
  210.9 51.7 %reduce-scatter.3.cloned.1.call-done = bf16[256,1280]{1,0:T(8,128)(2,1)} async-done(((bf16[1024,1280]{1,0:T(8,128)(2,1)}), bf16[256,1280]{1,0:T(8,128)(2,1)}) %reduce-scatter.3.cloned.1.call-update) | async-done | bytes 655376 | tf_op jit(solution)/shard_map/reduce_scatter | solution.py:91
  262.6 1.4 multiply_reduce_fusion
  264.0 6.2 %psum.14 = f32[256]{0:T(256)S(1)} all-reduce(f32[256]{0:T(256)S(1)} %multiply_reduce_fusion), channel_id=1, replica_groups=mesh['ga'=2,'aa'=4,'ba'=4] {'aa'}, use_global_device_ids=true, to_apply=%region_24.25 | all-reduce | flops 256 | bytes 2048 | tf_op jit(solution)/shard_map/psum | solution.py:97
  270.2 1.9 convolution_convert_fusion.1
  272.0 34.3 %all_to_all.24 = bf16[4,128,1280]{2,1,0:T(8,128)(2,1)} all-to-all(bf16[4,128,1280]{2,1,0:T(8,128)(2,1)S(1)} %bitcast.111), channel_id=1, replica_groups=mesh['ga'=2,'aa'=4,'ba'=4] {'ba'}, dimensions={0} | all-to-all | bytes 2621440 | tf_op jit(solution)/shard_map/all_to_all | solution.py:114
  306.4 39.6 %all-gather.11.cloned.1.call-done = bf16[512,5120]{1,0:T(8,128)(2,1)} async-done(((bf16[512,1280]{1,0:T(8,128)(2,1)}), bf16[512,5120]{1,0:T(8,128)(2,1)}) %all-gather.11.cloned.1.call-update) | async-done | bytes 5242896 | tf_op jit(solution)/shard_map/all_gather | solution.py:118
  346.1 9.9 %fusion.94 = f32[512,1024]{1,0:T(8,128)S(1)} fusion(bf16[512,5120]{1,0:T(8,128)(2,1)} %all-gather.11.cloned.1.call-done, bf16[1,5120,1024]{2,1,0:T(8,128)(2,1)} %param.26), kind=kOutput, calls=%fused_computation.121 | convolution fusion | flops 5368709120 | bytes 17825792 | tf_op jit(solution)/shard_map/dot_general | solution.py:120
  355.9 20.6 %fusion.101 = bf16[5120,512]{0,1:T(8,128)(2,1)} fusion(bf16[1,1024,5120]{2,1,0:T(8,128)(2,1)} %param.27, f32[512,1024]{1,0:T(8,128)S(1)} %fusion.94, bf16[512,5120]{1,0:T(8,128)(2,1)} %all-gather.11.cloned.1.call-done, bf16[1,5120,1024]{2,1,0:T(8,128)(2,1)} %param.25), kind=kOutput, calls=%fused_computation.126 | convolution fusion | flops 10743185408 | bytes 33554432 | tf_op jit(solution)/shard_map/dot_general | solution.py:123
  376.6 51.3 %reduce-scatter.5.cloned.1.call-done = bf16[1280,512]{0,1:T(8,128)(2,1)} async-done(((bf16[5120,512]{0,1:T(8,128)(2,1)}), bf16[1280,512]{0,1:T(8,128)(2,1)}) %reduce-scatter.5.cloned.1.call-update) | async-done | bytes 1310736 | tf_op jit(solution)/shard_map/reduce_scatter | solution.py:122
  427.9 4.6 all-to-all-start.1
  432.5 2.7 fusion.112
  435.2 6.1 %psum.15 = f32[256,4]{0,1:T(4,128)S(1)} all-reduce(f32[256,4]{0,1:T(4,128)S(1)} %fusion.112), channel_id=1, replica_groups=mesh['ga'=2,'aa'=4,'ba'=4] {'aa'}, use_global_device_ids=true, to_apply=%region_25.26 | all-reduce | flops 1024 | bytes 8192 | tf_op jit(solution)/shard_map/psum | solution.py:100
  441.3 22.4 %all-to-all-done.1 = bf16[1280,4,128]{0,2,1:T(8,128)(2,1)} async-done(((bf16[1280,4,128]{0,2,1:T(8,128)(2,1)}), bf16[1280,4,128]{0,2,1:T(8,128)(2,1)}, u32[]{:S(2)}, u32[]{:S(2)}) %all-to-all-start.1) | async-done | bytes 1310752 | tf_op jit(solution)/shard_map/all_to_all | solution.py:130
  463.8 3.1 fusion.105
  (171 shorter events, 47.8 us)
Async XLA Ops:
  6.5 196.7 %copy-start = (bf16[1280,1280]{1,0:T(8,128)(2,1)S(1)}, bf16[1280,1280]{1,0:T(8,128)(2,1)}, u32[]{:S(2)}) copy-start(bf16[1280,1280]{1,0:T(8,128)(2,1)} %param.20) | copy-start | bytes 9830404
  6.5 2.2 copy-start.11
  6.5 39.6 %all-gather.5.cloned.1.call-start = ((), (), s32[]{:S(2)}) async-start(), calls=%async_computation.4 | async-start | bytes 5242880 | tf_op jit(solution)/shard_map/all_gather | solution.py:77
  7.3 74.9 %all-gather.7.cloned.1.call-start = ((), (), s32[]{:S(2)}) async-start(), calls=%async_computation.5 | async-start | bytes 5242880 | tf_op jit(solution)/shard_map/all_gather | solution.py:78
  8.0 195.3 %all-gather.9.cloned.1.call-start = ((), (), s32[]{:S(2)}) async-start(), calls=%async_computation.6 | async-start | bytes 3276800 | tf_op jit(solution)/shard_map/all_gather | solution.py:90
  83.3 2.4 copy-start.2
  85.7 1.8 copy-start.5
  94.1 2.2 copy-start.3
  101.2 1.2 copy-start.4
  106.2 2.4 copy-start.2
  108.6 1.8 copy-start.5
  117.0 2.2 copy-start.3
  124.1 1.2 copy-start.4
  129.5 2.4 copy-start.2
  131.9 1.8 copy-start.5
  140.3 2.2 copy-start.3
  147.4 1.2 copy-start.4
  152.8 2.4 copy-start.2
  155.2 1.8 copy-start.5
  163.6 2.2 copy-start.3
  170.7 1.2 copy-start.4
  177.3 85.3 %reduce-scatter.3.cloned.1.call-start = ((), (), s32[]{:S(2)}) async-start(), calls=%async_computation.7 | async-start | bytes 3276800 | tf_op jit(solution)/shard_map/reduce_scatter | solution.py:91
  210.2 0.7 copy-start.8
  210.2 0.7 copy-start.7
  210.2 52.4 %copy-start.6 = (bf16[256,1280]{1,0:T(8,128)(2,1)S(1)}, bf16[256,1280]{1,0:T(8,128)(2,1)}, u32[]{:S(2)}) copy-start(bf16[256,1280]{1,0:T(8,128)(2,1)} %param.19) | copy-start | bytes 1966084
  210.2 60.0 %copy-start.10 = (f32[1280]{0:T(1024)S(1)}, f32[1280]{0:T(1024)}, u32[]{:S(2)}) copy-start(f32[1280]{0:T(1024)} %param.21) | copy-start | bytes 15364
  210.2 135.9 %all-gather.11.cloned.1.call-start = ((), (), s32[]{:S(2)}) async-start(), calls=%async_computation.8 | async-start | bytes 6553600 | tf_op jit(solution)/shard_map/all_gather | solution.py:118
  306.4 121.5 %reduce-scatter.5.cloned.1.call-start = ((), (), s32[]{:S(2)}) async-start(), calls=%async_computation.9 | async-start | bytes 6553600 | tf_op jit(solution)/shard_map/reduce_scatter | solution.py:122
  376.6 55.9 %copy-start.9 = (f32[1280,4]{0,1:T(4,128)S(1)}, f32[1280,4]{0,1:T(4,128)}, u32[]{:S(2)}) copy-start(f32[1280,4]{0,1:T(4,128)} %param.22) | copy-start | bytes 61444
  427.9 35.9 %all-to-all-start.1 = ((bf16[1280,4,128]{0,2,1:T(8,128)(2,1)}), bf16[1280,4,128]{0,2,1:T(8,128)(2,1)}, u32[]{:S(2)}, u32[]{:S(2)}) async-start(bf16[1280,4,128]{0,2,1:T(8,128)(2,1)} %bitcast.110), calls=%async_computation.3 | async-start | bytes 2621440 | tf_op jit(solution)/shard_map/all_to_all | solution.py:130
  432.5 34.4 %copy-start.1 = (bf16[1280,1280]{1,0:T(8,128)(2,1)S(1)}, bf16[1280,1280]{1,0:T(8,128)(2,1)}, u32[]{:S(2)}) copy-start(bf16[1280,1280]{1,0:T(8,128)(2,1)} %param.20) | copy-start | bytes 9830404
Sparse Core Ops, SparseCore 0:
  8.9 37.1 all-gather.4
  47.7 34.4 all-gather.6
  177.4 25.8 all-gather.8
  210.3 52.2 reduce-scatter.2
  306.5 39.5 all-gather.10
  376.7 51.1 reduce-scatter.4
where the time goes:
time: 475 us; the launch traced here: 474 us
  waiting for transfers between devices  258 us (54%)
  matrix products  96 us (20%)
  blocking collectives  53 us (11%)
  other arithmetic  32.1 us (7%)
  local copies, waits for them, and re-layouts  14.9 us (3%)
  between operations  14.2 us (3%)
  starting transfers between devices  4.8 us (1%)
    reduce_scatter x1, waiting for transfers between devices, on_device(): lax.psum_scatter(jnp.dot(attended, out_weight, preferred_element_type=jnp...  51.7 us
    reduce_scatter x1, waiting for transfers between devices, on_device(): lax.psum_scatter(lax.dot_general(down_w, act, (((0,), (1,)), ((), ())), p...  51.3 us
    all_gather x1, waiting for transfers between devices, on_device(): piece = lax.all_gather(arrived, 'aa', axis=1, tiled=True)  39.6 us
    all_gather x1, waiting for transfers between devices, on_device(): value_piece = lax.all_gather(values, 'aa', axis=0, tiled=True)  36 us
    all_to_all x1, blocking collectives, on_device(): lax.all_to_all(packed, 'ba', split_axis=0, concat_axis=0, tiled=True)  34.3 us
    dot_general x40, matrix products, head_partials(): lax.dot_general(q_head, k_head, (((1,), (1,)), ((), ())), preferred_eleme...  31.6 us
    all_gather x1, waiting for transfers between devices, on_device(): key_piece = lax.all_gather(keys, 'aa', axis=0, tiled=True)  29.7 us
    all_gather x1, waiting for transfers between devices, on_device(): attended = lax.all_gather(own, 'aa', axis=0, tiled=True)  26 us
  transfers between devices with their start and end apart: 7, of which 7 were waited for; matrix products, arithmetic and copies ran while one was open for 1% of the time, Pallas kernels for 0%

commit v1 on v0

v1 whole, which is shorter than its diff:
```python
import functools

import jax
import jax.numpy as jnp
from jax import lax
from jax.experimental import pallas as pl
from jax.experimental.pallas import tpu as pltpu
from jax.sharding import PartitionSpec as P

D = 5120
HD = 128
Q = 1024
STEP = 512
LOG2E = 1.4426950408889634


NEGATIVE = -1e30
EPSILON = 1e-05


def attend_kernel(shards, group, lengths, q_ref, *refs):
    key_refs = refs[:shards]
    value_refs = refs[shards : 2 * shards]
    out_ref, stat_ref, peak_ref, total_ref, acc_ref = refs[2 * shards :]
    factor = HD ** (-0.5) * LOG2E
    context = key_refs[0].shape[0]
    step = min(STEP, context)
    peak_ref[...] = jnp.full_like(peak_ref, NEGATIVE)
    total_ref[...] = jnp.zeros_like(total_ref)
    acc_ref[...] = jnp.zeros_like(acc_ref)

    def chunk(shard, start, limit):
        k = key_refs[shard][pl.ds(start, step), :]
        v = value_refs[shard][pl.ds(start, step), :]
        for head in range(group):
            q = q_ref[:, head * HD : (head + 1) * HD]
            scores = lax.dot_general(
                k, q, (((1,), (1,)), ((), ())), preferred_element_type=jnp.float32
            )
            if limit is not None:
                place = lax.broadcasted_iota(jnp.int32, scores.shape, 0)
                scores = jnp.where(place < limit, scores, NEGATIVE)
            old = peak_ref[head : head + 1, :]
            new = jnp.maximum(old, jnp.max(scores, axis=0, keepdims=True))
            probs = jnp.exp2((scores - new) * factor)
            scale = jnp.exp2((old - new) * factor)
            peak_ref[head : head + 1, :] = new
            total_ref[head : head + 1, :] = total_ref[head : head + 1, :] * scale + jnp.sum(
                probs, axis=0, keepdims=True
            )
            acc_ref[head] = acc_ref[head] * scale + lax.dot_general(
                v,
                probs.astype(jnp.bfloat16),
                (((0,), (0,)), ((), ())),
                preferred_element_type=jnp.float32,
            )

    for shard in range(shards):
        length = lengths[shard]
        full = length // step

        @pl.loop(0, full)
        def _(i, shard=shard):
            chunk(shard, pl.multiple_of(i * step, step), None)

        @pl.when(length > full * step)
        def _(shard=shard, full=full, length=length):
            chunk(shard, pl.multiple_of(full * step, step), length - full * step)

    for head in range(group):
        total = total_ref[head : head + 1, :]
        out_ref[:, head * HD : (head + 1) * HD] = jnp.transpose(acc_ref[head] / total).astype(
            out_ref.dtype
        )
    stat_ref[0, 0] = peak_ref[...]
    stat_ref[0, 1] = total_ref[...]


def attend(query, key_blocks, value_blocks, lengths, out_type):
    shards = len(key_blocks)
    rows, width = query.shape
    kv_heads = key_blocks[0].shape[1] // HD
    group = width // HD // kv_heads
    context = key_blocks[0].shape[0]
    kv_spec = pl.BlockSpec((context, HD), lambda g, n: (0, g))
    work = shards * rows * width * context
    return pl.pallas_call(
        functools.partial(attend_kernel, shards, group),
        grid_spec=pltpu.PrefetchScalarGridSpec(
            num_scalar_prefetch=1,
            grid=(kv_heads,),
            in_specs=[pl.BlockSpec((rows, group * HD), lambda g, n: (0, g))]
            + [kv_spec] * (2 * shards),
            out_specs=[
                pl.BlockSpec((rows, group * HD), lambda g, n: (0, g)),
                pl.BlockSpec((1, 2, group, rows), lambda g, n: (g, 0, 0, 0)),
            ],
            scratch_shapes=[
                pltpu.VMEM((group, rows), jnp.float32),
                pltpu.VMEM((group, rows), jnp.float32),
                pltpu.VMEM((group, HD, rows), jnp.float32),
            ],
        ),
        out_shape=[
            jax.ShapeDtypeStruct((rows, width), out_type),
            jax.ShapeDtypeStruct((kv_heads, 2, group, rows), jnp.float32),
        ],
        cost_estimate=pl.CostEstimate(
            flops=8 * work, bytes_accessed=4 * shards * context * kv_heads * HD + 6 * rows * width,
            transcendentals=work // HD,
        ),
        compiler_params=pltpu.CompilerParams(vmem_limit_bytes=32 * 1024 * 1024),
        name="attend",
    )(lengths, query, *key_blocks, *value_blocks)


def span_attention(query, keys, values, cache_lengths):
    size = lax.axis_size("aa")
    swap = [(i, i ^ 1) for i in range(size)]
    far = []
    for hop in range(2, size, 2):
        ahead = [(i, (i + hop) % size) for i in range(size)]
        far.append((lax.ppermute(query, "aa", ahead), [(j, i) for i, j in ahead]))
    near_keys = lax.ppermute(keys, "aa", swap)
    near_values = lax.ppermute(values, "aa", swap)
    near_length = lax.ppermute(cache_lengths, "aa", swap)
    both = jnp.concatenate([cache_lengths, near_length])
    parts = [attend(query, [keys], [values], cache_lengths, jnp.float32)]
    for rows, back in far:
        out, stat = attend(rows, [keys, near_keys], [values, near_values], both, jnp.bfloat16)
        parts.append((lax.ppermute(out, "aa", back), lax.ppermute(stat, "aa", back)))
    parts.append(attend(query, [near_keys], [near_values], near_length, jnp.float32))
    peaks = [stat[:, 0] for _, stat in parts]
    top = functools.reduce(jnp.maximum, peaks)
    weights = [
        stat[:, 1] * jnp.exp((stat[:, 0] - top) * HD ** (-0.5)) for _, stat in parts
    ]
    whole = functools.reduce(jnp.add, weights)
    rows, width = query.shape
    total = 0.0
    for (out, _), weight in zip(parts, weights):
        share = (weight / whole).reshape(width // HD, rows).T
        total = total + out.astype(jnp.float32).reshape(rows, width // HD, HD) * share[:, :, None]
    return total.reshape(rows, width).astype(jnp.bfloat16)


def on_device(
    query,
    keys,
    values,
    cache_lengths,
    residual,
    out_weight,
    norm_gain,
    router_weight,
    expert_ids,
    expert_slots,
    expert_gate,
    expert_up,
    expert_down,
):
    own = span_attention(query, keys, values, cache_lengths)
    attended = lax.all_gather(own, "aa", axis=0, tiled=True)
    hidden = residual.astype(jnp.float32) + lax.psum_scatter(
        jnp.dot(attended, out_weight, preferred_element_type=jnp.float32).astype(jnp.bfloat16),
        "ba",
        scatter_dimension=0,
        tiled=True,
    ).astype(jnp.float32)
    scaled = hidden * norm_gain
    sums = lax.psum(
        jnp.concatenate(
            [
                jnp.dot(scaled, router_weight, precision=lax.Precision.HIGHEST),
                jnp.sum(hidden * hidden, axis=1, keepdims=True),
            ],
            axis=1,
        ),
        "aa",
    )
    inverse = 1.0 / jnp.sqrt(sums[:, -1] / D + EPSILON)
    normed = scaled * inverse[:, None]
    logits = sums[:, :-1] * inverse[:, None]
    experts = router_weight.shape[1]
    chosen = expert_ids[:, None] == lax.broadcasted_iota(jnp.int32, (1, experts), 1)
    gate = jnp.sum(jnp.where(chosen, jax.nn.sigmoid(logits), 0.0), axis=1)
    expert_in = normed.astype(jnp.bfloat16)
    slot_count = 2 * Q // (lax.axis_size("ba") * experts)
    combined = expert_ids * slot_count + expert_slots
    placing = (
        combined[:, None] == lax.broadcasted_iota(jnp.int32, (1, experts * slot_count), 1)
    ) & (expert_slots[:, None] >= 0)
    placing = placing.astype(jnp.bfloat16)
    packed = lax.dot_general(
        placing, expert_in, (((0,), (0,)), ((), ())), preferred_element_type=jnp.float32
    ).astype(jnp.bfloat16)
    arrived = lax.all_to_all(packed, "ba", split_axis=0, concat_axis=0, tiled=True)
    gate_w = expert_gate[0]
    up_w = expert_up[0]
    down_w = expert_down[0]
    piece = lax.all_gather(arrived, "aa", axis=1, tiled=True)
    gate_part = jnp.dot(piece, gate_w, preferred_element_type=jnp.float32)
    up_part = jnp.dot(piece, up_w, preferred_element_type=jnp.float32)
    act = (jax.nn.silu(gate_part) * up_part).astype(jnp.bfloat16)
    expert_out = lax.psum_scatter(
        lax.dot_general(
            down_w, act, (((0,), (1,)), ((), ())), preferred_element_type=jnp.float32
        ).astype(jnp.bfloat16),
        "aa",
        scatter_dimension=0,
        tiled=True,
    )
    returned = lax.all_to_all(expert_out, "ba", split_axis=1, concat_axis=1, tiled=True)
    from_experts = lax.dot_general(
        placing, returned, (((1,), (1,)), ((), ())), preferred_element_type=jnp.float32
    )
    return (hidden + gate[:, None] * from_experts).astype(jnp.bfloat16)


def solution(mesh):
    return jax.shard_map(
        on_device,
        mesh=mesh,
        in_specs=(
            P(("ga", "aa"), "ba"),
            P(("ga", "aa"), "ba"),
            P(("ga", "aa"), "ba"),
            P(("ga", "aa")),
            P(("ga", "ba"), "aa"),
            P("ba", "aa"),
            P("aa"),
            P("aa", None),
            P(("ga", "ba")),
            P(("ga", "ba")),
            P("ba", None, "aa"),
            P("ba", None, "aa"),
            P("ba", "aa", None),
        ),
        out_specs=P(("ga", "ba"), "aa"),
        check_vma=False,
    )
```

time: 475 us -> 413 us (0.87)
  matrix products: 96 us -> 42.5 us
  Pallas kernels: 0 us -> 49 us
  waiting for transfers between devices: 258 us -> 222 us
  other arithmetic: 32.1 us -> 6.67 us
  blocking collectives: 53 us -> 40.6 us
  starting transfers between devices: 4.8 us -> 17.1 us
  local copies, waits for them, and re-layouts: 14.9 us -> 20.7 us
    all_gather x2 -> x0, waiting for transfers between devices: 65.7 us -> none  [the longest x1 36 us: on_device(): value_piece = lax.all_gather(values, 'aa', axis=0, tiled=True)]
    dot_general x81 -> x1, matrix products: 53.7 us -> 1.21 us  [on_device(): jnp.dot(scaled, router_weight, precision=lax.Precision.HIGHEST)]
    pallas_call x0 -> x3, Pallas kernels: none -> 49 us  [attend(): pl.pallas_call(functools.partial(attend_kernel, shards, group), grid_spec...]
    all_gather x1, waiting for transfers between devices: 26 us -> 44.6 us  [on_device(): attended = lax.all_gather(own, 'aa', axis=0, tiled=True)]
    reduce_sum x41 -> x1, other arithmetic: 15.8 us -> 1.45 us  [on_device(): jnp.sum(hidden * hidden, axis=1, keepdims=True)]
    ppermute x0 -> x6, starting transfers between devices: none -> 12.4 us  [the longest x1 4.56 us: span_attention(): lax.ppermute(stat, 'aa', back)]
    mul x0 -> x6, local copies, waits for them, and re-layouts: none -> 11.9 us  [span_attention(): out.astype(jnp.float32).reshape(rows, width // HD, HD) * share[:, :, None]]
    add x8 -> x0, other arithmetic: 11.7 us -> none  [the longest x4 11.6 us: combine_partials(): out_one * jnp.repeat(scale_one, HD, axis=1)]
  transfers between devices with their start and end apart: 7 -> 11, of which waited for: 7 -> 6; matrix products, arithmetic and copies ran while one was open for 1% -> 3% of each run, Pallas kernels for 0% -> 6%
where the time goes in v1:
time: 413 us; the launch traced here: 412 us
  waiting for transfers between devices  222 us (54%)
  Pallas kernels  49 us (12%)
  matrix products  42.5 us (10%)
  blocking collectives  40.6 us (10%)
  local copies, waits for them, and re-layouts  20.7 us (5%)
  starting transfers between devices  17.1 us (4%)
  between operations  14 us (3%)
  other arithmetic  6.67 us (2%)
    reduce_scatter x1, waiting for transfers between devices, on_device(): lax.psum_scatter(jnp.dot(attended, out_weight, preferred_element_type=jnp...  51.7 us
    reduce_scatter x1, waiting for transfers between devices, on_device(): lax.psum_scatter(lax.dot_general(down_w, act, (((0,), (1,)), ((), ())), p...  51.3 us
    pallas_call x3, Pallas kernels, attend(): pl.pallas_call(functools.partial(attend_kernel, shards, group), grid_spec...  49 us
    all_gather x1, waiting for transfers between devices, on_device(): attended = lax.all_gather(own, 'aa', axis=0, tiled=True)  44.6 us
    all_gather x1, waiting for transfers between devices, on_device(): piece = lax.all_gather(arrived, 'aa', axis=1, tiled=True)  39.6 us
    all_to_all x1, blocking collectives, on_device(): lax.all_to_all(packed, 'ba', split_axis=0, concat_axis=0, tiled=True)  34.3 us
    all_to_all x1, waiting for transfers between devices, on_device(): lax.all_to_all(expert_out, 'ba', split_axis=1, concat_axis=1, tiled=True)  31.3 us
    dot_general x1, matrix products, on_device(): lax.dot_general(down_w, act, (((0,), (1,)), ((), ())), preferred_element_...  20.6 us
  transfers between devices with their start and end apart: 11, of which 6 were waited for; matrix products, arithmetic and copies ran while one was open for 3% of the time, Pallas kernels for 6%

profile of v1, /device:TPU:0, one launch (start us, length us, event | category | flops | bytes accessed | tf_op | source)
XLA Modules:
  0.0 412.4 jit_solution(1282267285805524184)
XLA Ops:
  6.5 0.0 copy-start
  6.5 0.0 all-gather.3.cloned.1.call-start
  6.5 0.5 collective-permute-start.2
  7.0 0.0 collective-permute-start.3
  7.1 0.5 collective-permute-start
  7.5 2.5 collective-permute-start.1
  10.7 0.0 copy-start.4
  10.7 1.2 copy-done.4
  11.9 1.2 copy-done.6
  13.1 1.1 copy-done.8
  14.2 18.1 %attend.3 = (f32[256,1280]{1,0:T(8,128)S(1)}, f32[2,2,5,256]{3,2,1,0:T(8,128)S(1)}) custom-call(s32[1]{0:T(128)S(6)} %copy.20.lengths, bf16[256,1280]{1,0:T(8,128)(2,1)S(1)} %copy-done.8, bf16[2048,256]{1,0:T(8,128)(2,1)S(1)} %copy-done.4, bf16[2048,256]{1,0:T(8,128)(2,1)S(1)} %copy-done.6), custom_call_target="tpu_custom_call" | custom-call | flops 5368709120 | bytes 4063232 | tf_op jit(solution)/shard_map/attend/pallas_call | solution.py:87
  32.4 0.0 copy-start.2
  32.4 1.1 copy-done.2
  33.5 0.0 collective-permute-done.lengths
  33.5 0.8 pad_add_fusion.lengths
  34.2 0.0 collective-permute-done.1.q_ref
  34.2 0.0 collective-permute-done.2.refs_1_.refs_0_
  34.2 0.0 collective-permute-done.3.refs_3_.refs_1_
  34.3 0.0 copy-start.5
  34.3 1.2 copy-done.5
  35.5 1.2 copy-done.7
  36.7 23.8 %attend.4 = (bf16[256,1280]{1,0:T(8,128)(2,1)S(1)}, f32[2,2,5,256]{3,2,1,0:T(8,128)S(1)}) custom-call(s32[2]{0:T(128)S(1)} %pad_add_fusion.lengths, bf16[256,1280]{1,0:T(8,128)(2,1)} %collective-permute-done.1.q_ref, bf16[2048,256]{1,0:T(8,128)(2,1)S(1)} %copy-done.5, bf16[2048,256]{1,0:T(8,128)(2,1)} %collective-permute-done.2.refs_1_.refs_0_, ...), custom_call_target="tpu_custom_call" | custom-call | flops 10737418240 | bytes 6160384 | tf_op jit(solution)/shard_map/attend/pallas_call | solution.py:87
  60.5 0.0 copy-start.10
  60.5 4.6 %collective-permute-start.4 = (f32[2,2,5,256]{3,2,1,0:T(8,128)S(1)}, f32[2,2,5,256]{3,2,1,0:T(8,128)S(1)}, u32[]{:S(2)}, u32[]{:S(2)}) collective-permute-start(f32[2,2,5,256]{3,2,1,0:T(8,128)S(1)} %get-tuple-element.13), channel_id=1, source_target_pairs={{8,0},{12,4},{0,8},{4,12},{9,1},{13,5},{1,9},{5,13},{10,2},{14,6},... | collective-permute-start | bytes 61448 | tf_op jit(solution)/shard_map/ppermute | solution.py:131
  65.1 0.0 copy-done.9
  65.1 7.0 %attend.5 = (f32[256,1280]{1,0:T(8,128)S(1)}, f32[2,2,5,256]{3,2,1,0:T(8,128)S(1)}) custom-call(s32[1]{0:T(128)} %collective-permute-done.lengths, bf16[256,1280]{1,0:T(8,128)(2,1)S(1)} %copy-done.9, bf16[2048,256]{1,0:T(8,128)(2,1)} %collective-permute-done.2.refs_1_.refs_0_, bf16[2048,256]{1,0:T(8,128)(2,1)} %collective-permute-done.3.refs_3_.refs_1_), custom_call_target="tpu_custom_call" | custom-call | flops 5368709120 | bytes 4063232 | tf_op jit(solution)/shard_map/attend/pallas_call | solution.py:87
  72.1 1.1 copy-done.3
  73.2 4.4 %collective-permute-start.5 = (bf16[256,1280]{1,0:T(8,128)(2,1)}, bf16[256,1280]{1,0:T(8,128)(2,1)}, u32[]{:S(2)}, u32[]{:S(2)}) collective-permute-start(bf16[256,1280]{1,0:T(8,128)(2,1)} %copy-done.10), channel_id=1, source_target_pairs={{8,0},{12,4},{0,8},{4,12},{9,1},{13,5},{1,9},{5,13},{10,2},{14,6},... | collective-permute-start | bytes 1966088 | tf_op jit(solution)/shard_map/ppermute | solution.py:131
  77.6 0.0 collective-permute-done.4
  77.6 1.2 mul.128
  78.8 2.8 copy.18
  81.6 1.2 mul.125
  82.8 2.8 copy.17
  85.6 1.2 mul.131
  86.8 2.8 copy.19
  89.6 3.3 collective-permute-done.5
  92.8 4.3 %add_convert_fusion = bf16[256,1280]{1,0:T(8,128)(2,1)} fusion(f32[256,1280]{1,0:T(8,128)} %copy-done.3, f32[256,1280]{1,0:T(8,128)} %copy.19, f32[256,1280]{1,0:T(8,128)} %copy.18, bf16[256,1280]{1,0:T(8,128)(2,1)} %collective-permute-done.5, f32[256,1280]{1,0:T(8,128)} %copy-done.2, f32[256,1280]{1,0:T(8,128)} %copy.17), kind=kLoop, calls=%fused_computation.17 | loop fusion | flops 2293760 | bytes 7864320 | tf_op jit(solution)/shard_map/convert_element_type | solution.py:144
  97.2 0.0 all-gather.3.cloned.1.call-update
  97.2 0.0 reduce-scatter.3.cloned.1.call-start
  97.3 44.6 %all-gather.3.cloned.1.call-done = bf16[1024,1280]{1,0:T(8,128)(2,1)} async-done(((bf16[256,1280]{1,0:T(8,128)(2,1)}), bf16[1024,1280]{1,0:T(8,128)(2,1)}) %all-gather.3.cloned.1.call-update) | async-done | bytes 2621456 | tf_op jit(solution)/shard_map/all_gather | solution.py:163
  141.9 6.8 %convolution_convert_fusion = bf16[1024,1280]{1,0:T(8,128)(2,1)} fusion(bf16[1024,1280]{1,0:T(8,128)(2,1)} %all-gather.3.cloned.1.call-done, bf16[1280,1280]{1,0:T(8,128)(2,1)S(1)} %copy-done), kind=kOutput, calls=%fused_computation.8 | convolution fusion | flops 3356753920 | bytes 8519680 | tf_op jit(solution)/shard_map/dot_general | solution.py:165
  148.7 0.0 reduce-scatter.3.cloned.1.call-update
  148.7 0.0 copy-start.13
  148.8 0.0 copy-start.14
  148.8 0.0 all-gather.5.cloned.1.call-start
  148.8 0.6 copy-done.16
  149.4 0.0 copy-done.15
  149.4 51.7 %reduce-scatter.3.cloned.1.call-done = bf16[256,1280]{1,0:T(8,128)(2,1)} async-done(((bf16[1024,1280]{1,0:T(8,128)(2,1)}), bf16[256,1280]{1,0:T(8,128)(2,1)}) %reduce-scatter.3.cloned.1.call-update) | async-done | bytes 655376 | tf_op jit(solution)/shard_map/reduce_scatter | solution.py:164
  201.2 0.0 copy-done.11
  201.2 1.4 multiply_reduce_fusion
  202.6 1.2 fusion.18
  203.9 6.3 %psum.7 = f32[256,5]{0,1:T(8,128)S(1)} all-reduce(f32[256,5]{0,1:T(8,128)S(1)} %pad_maximum_fusion), channel_id=1, replica_groups=mesh['ga'=2,'aa'=4,'ba'=4] {'aa'}, use_global_device_ids=true, to_apply=%region_2.0 | all-reduce | flops 1280 | bytes 10240 | tf_op jit(solution)/shard_map/psum | solution.py:171
  210.2 0.8 convolution_convert_fusion.1
  211.0 34.3 %all_to_all.24 = bf16[4,128,1280]{2,1,0:T(8,128)(2,1)} all-to-all(bf16[4,128,1280]{2,1,0:T(8,128)(2,1)S(1)} %bitcast.45), channel_id=1, replica_groups=mesh['ga'=2,'aa'=4,'ba'=4] {'ba'}, dimensions={0} | all-to-all | bytes 2621440 | tf_op jit(solution)/shard_map/all_to_all | solution.py:197
  245.3 0.0 all-gather.5.cloned.1.call-update
  245.3 0.0 reduce-scatter.5.cloned.1.call-start
  245.3 39.6 %all-gather.5.cloned.1.call-done = bf16[512,5120]{1,0:T(8,128)(2,1)} async-done(((bf16[512,1280]{1,0:T(8,128)(2,1)}), bf16[512,5120]{1,0:T(8,128)(2,1)}) %all-gather.5.cloned.1.call-update) | async-done | bytes 5242896 | tf_op jit(solution)/shard_map/all_gather | solution.py:201
  284.9 9.8 %fusion.2 = f32[512,1024]{1,0:T(8,128)S(1)} fusion(bf16[512,5120]{1,0:T(8,128)(2,1)} %all-gather.5.cloned.1.call-done, bf16[1,5120,1024]{2,1,0:T(8,128)(2,1)} %param.24), kind=kOutput, calls=%fused_computation.2 | convolution fusion | flops 5368709120 | bytes 17825792 | tf_op jit(solution)/shard_map/dot_general | solution.py:203
  294.8 20.6 %fusion.9 = bf16[5120,512]{0,1:T(8,128)(2,1)} fusion(bf16[1,1024,5120]{2,1,0:T(8,128)(2,1)} %param.25, f32[512,1024]{1,0:T(8,128)S(1)} %fusion.2, bf16[512,5120]{1,0:T(8,128)(2,1)} %all-gather.5.cloned.1.call-done, bf16[1,5120,1024]{2,1,0:T(8,128)(2,1)} %param.23), kind=kOutput, calls=%fused_computation.7 | convolution fusion | flops 10743185408 | bytes 33554432 | tf_op jit(solution)/shard_map/dot_general | solution.py:206
  315.4 0.0 reduce-scatter.5.cloned.1.call-update
  315.4 51.3 %reduce-scatter.5.cloned.1.call-done = bf16[1280,512]{0,1:T(8,128)(2,1)} async-done(((bf16[5120,512]{0,1:T(8,128)(2,1)}), bf16[1280,512]{0,1:T(8,128)(2,1)}) %reduce-scatter.5.cloned.1.call-update) | async-done | bytes 1310736 | tf_op jit(solution)/shard_map/reduce_scatter | solution.py:205
  366.8 4.6 %all-to-all-start.1 = ((bf16[1280,4,128]{0,2,1:T(8,128)(2,1)}), bf16[1280,4,128]{0,2,1:T(8,128)(2,1)}, u32[]{:S(2)}, u32[]{:S(2)}) async-start(bf16[1280,4,128]{0,2,1:T(8,128)(2,1)} %bitcast.44), calls=%async_computation.3 | async-start | bytes 2621440 | tf_op jit(solution)/shard_map/all_to_all | solution.py:213
  371.4 31.3 %all-to-all-done.1 = bf16[1280,4,128]{0,2,1:T(8,128)(2,1)} async-done(((bf16[1280,4,128]{0,2,1:T(8,128)(2,1)}), bf16[1280,4,128]{0,2,1:T(8,128)(2,1)}, u32[]{:S(2)}, u32[]{:S(2)}) %all-to-all-start.1) | async-done | bytes 1310752 | tf_op jit(solution)/shard_map/all_to_all | solution.py:213
  402.7 3.2 fusion.13
  (32 shorter events, 0.2 us)
Async XLA Ops:
  6.5 135.4 %copy-start = (bf16[1280,1280]{1,0:T(8,128)(2,1)S(1)}, bf16[1280,1280]{1,0:T(8,128)(2,1)}, u32[]{:S(2)}) copy-start(bf16[1280,1280]{1,0:T(8,128)(2,1)} %param.18) | copy-start | bytes 9830404
  6.5 135.4 %all-gather.3.cloned.1.call-start = ((), (), s32[]{:S(2)}) async-start(), calls=%async_computation.4 | async-start | bytes 3276800 | tf_op jit(solution)/shard_map/all_gather | solution.py:163
  6.5 27.7 %collective-permute-start.2 = (bf16[2048,256]{1,0:T(8,128)(2,1)}, bf16[2048,256]{1,0:T(8,128)(2,1)}, u32[]{:S(2)}, u32[]{:S(2)}) collective-permute-start(bf16[2048,256]{1,0:T(8,128)(2,1)} %refs_0_.3), channel_id=1, source_target_pairs={{0,4},{4,0},{8,12},{12,8},{1,5},{5,1},{9,13},{13,9},{2,6},{6,2},{1... | collective-permute-start | bytes 3145736 | tf_op jit(solution)/shard_map/ppermute | solution.py:124
  7.0 27.2 %collective-permute-start.3 = (bf16[2048,256]{1,0:T(8,128)(2,1)}, bf16[2048,256]{1,0:T(8,128)(2,1)}, u32[]{:S(2)}, u32[]{:S(2)}) collective-permute-start(bf16[2048,256]{1,0:T(8,128)(2,1)} %refs_2_.1), channel_id=1, source_target_pairs={{0,4},{4,0},{8,12},{12,8},{1,5},{5,1},{9,13},{13,9},{2,6},{6,2},{1... | collective-permute-start | bytes 3145736 | tf_op jit(solution)/shard_map/ppermute | solution.py:125
  7.1 26.4 %collective-permute-start = (s32[1]{0:T(128)}, s32[1]{0:T(128)}, u32[]{:S(2)}, u32[]{:S(2)}) collective-permute-start(s32[1]{0:T(128)} %param.16), channel_id=1, source_target_pairs={{0,4},{4,0},{8,12},{12,8},{1,5},{5,1},{9,13},{13,9},{2,6},{6,2},{1... | collective-permute-start | bytes 20 | tf_op jit(solution)/shard_map/ppermute | solution.py:126
  7.5 26.7 %collective-permute-start.1 = (bf16[256,1280]{1,0:T(8,128)(2,1)}, bf16[256,1280]{1,0:T(8,128)(2,1)}, u32[]{:S(2)}, u32[]{:S(2)}) collective-permute-start(bf16[256,1280]{1,0:T(8,128)(2,1)} %q_ref.3), channel_id=1, source_target_pairs={{0,8},{4,12},{8,0},{12,4},{1,9},{5,13},{9,1},{13,5},{2,10},{6,14},... | collective-permute-start | bytes 1966088 | tf_op jit(solution)/shard_map/ppermute | solution.py:123
  10.7 1.2 copy-start.4
  11.9 1.2 copy-start.6
  13.1 1.1 copy-start.8
  32.4 1.1 copy-start.2
  34.3 1.2 copy-start.5
  35.5 1.2 copy-start.7
  36.7 28.4 %copy-start.9 = (bf16[256,1280]{1,0:T(8,128)(2,1)S(1)}, bf16[256,1280]{1,0:T(8,128)(2,1)}, u32[]{:S(2)}) copy-start(bf16[256,1280]{1,0:T(8,128)(2,1)} %q_ref.3) | copy-start | bytes 1966084
  60.5 11.6 %copy-start.10 = (bf16[256,1280]{1,0:T(8,128)(2,1)}, bf16[256,1280]{1,0:T(8,128)(2,1)S(1)}, u32[]{:S(2)}) copy-start(bf16[256,1280]{1,0:T(8,128)(2,1)S(1)} %get-tuple-element.15) | copy-start | bytes 1966084
  60.5 17.1 %collective-permute-start.4 = (f32[2,2,5,256]{3,2,1,0:T(8,128)S(1)}, f32[2,2,5,256]{3,2,1,0:T(8,128)S(1)}, u32[]{:S(2)}, u32[]{:S(2)}) collective-permute-start(f32[2,2,5,256]{3,2,1,0:T(8,128)S(1)} %get-tuple-element.13), channel_id=1, source_target_pairs={{8,0},{12,4},{0,8},{4,12},{9,1},{13,5},{1,9},{5,13},{10,2},{14,6},... | collective-permute-start | bytes 61448 | tf_op jit(solution)/shard_map/ppermute | solution.py:131
  72.1 1.1 copy-start.3
  73.2 19.6 %collective-permute-start.5 = (bf16[256,1280]{1,0:T(8,128)(2,1)}, bf16[256,1280]{1,0:T(8,128)(2,1)}, u32[]{:S(2)}, u32[]{:S(2)}) collective-permute-start(bf16[256,1280]{1,0:T(8,128)(2,1)} %copy-done.10), channel_id=1, source_target_pairs={{8,0},{12,4},{0,8},{4,12},{9,1},{13,5},{1,9},{5,13},{10,2},{14,6},... | collective-permute-start | bytes 1966088 | tf_op jit(solution)/shard_map/ppermute | solution.py:131
  97.2 103.9 %reduce-scatter.3.cloned.1.call-start = ((), (), s32[]{:S(2)}) async-start(), calls=%async_computation.5 | async-start | bytes 3276800 | tf_op jit(solution)/shard_map/reduce_scatter | solution.py:164
  148.7 0.7 copy-start.16
  148.7 0.7 copy-start.15
  148.7 52.4 %copy-start.11 = (bf16[256,1280]{1,0:T(8,128)(2,1)S(1)}, bf16[256,1280]{1,0:T(8,128)(2,1)}, u32[]{:S(2)}) copy-start(bf16[256,1280]{1,0:T(8,128)(2,1)} %param.17) | copy-start | bytes 1966084
  148.7 53.9 %copy-start.13 = (f32[1280,4]{0,1:T(4,128)S(1)}, f32[1280,4]{0,1:T(4,128)}, u32[]{:S(2)}) copy-start(f32[1280,4]{0,1:T(4,128)} %param.20) | copy-start | bytes 61444
  148.8 53.9 %copy-start.14 = (f32[1280]{0:T(1024)S(1)}, f32[1280]{0:T(1024)}, u32[]{:S(2)}) copy-start(f32[1280]{0:T(1024)} %param.19) | copy-start | bytes 15364
  148.8 136.2 %all-gather.5.cloned.1.call-start = ((), (), s32[]{:S(2)}) async-start(), calls=%async_computation.6 | async-start | bytes 6553600 | tf_op jit(solution)/shard_map/all_gather | solution.py:201
  201.2 1.5 copy-start.12
  245.3 121.5 %reduce-scatter.5.cloned.1.call-start = ((), (), s32[]{:S(2)}) async-start(), calls=%async_computation.7 | async-start | bytes 6553600 | tf_op jit(solution)/shard_map/reduce_scatter | solution.py:205
  366.8 35.9 %all-to-all-start.1 = ((bf16[1280,4,128]{0,2,1:T(8,128)(2,1)}), bf16[1280,4,128]{0,2,1:T(8,128)(2,1)}, u32[]{:S(2)}, u32[]{:S(2)}) async-start(bf16[1280,4,128]{0,2,1:T(8,128)(2,1)} %bitcast.44), calls=%async_computation.3 | async-start | bytes 2621440 | tf_op jit(solution)/shard_map/all_to_all | solution.py:213
  402.7 3.2 copy-start.1
Sparse Core Ops, SparseCore 0:
  97.3 44.5 all-gather.2
  148.9 52.2 reduce-scatter.2
  245.4 39.4 all-gather.4
  315.6 51.1 reduce-scatter.4

commit v2 on v1

--- a/solution.py
+++ b/solution.py
@@ -11,6 +11,7 @@
 HD = 128
 Q = 1024
 STEP = 512
+LANES = 128
 LOG2E = 1.4426950408889634
 
 
@@ -130,18 +131,245 @@
         out, stat = attend(rows, [keys, near_keys], [values, near_values], both, jnp.bfloat16)
         parts.append((lax.ppermute(out, "aa", back), lax.ppermute(stat, "aa", back)))
     parts.append(attend(query, [near_keys], [near_values], near_length, jnp.float32))
-    peaks = [stat[:, 0] for _, stat in parts]
-    top = functools.reduce(jnp.maximum, peaks)
-    weights = [
-        stat[:, 1] * jnp.exp((stat[:, 0] - top) * HD ** (-0.5)) for _, stat in parts
-    ]
+    return merge(parts, keys.shape[1] // HD)
+
+
+def merge_kernel(count, group, *refs):
+    stats, outs, out_ref = refs[:count], refs[count : 2 * count], refs[-1]
+    factor = HD ** (-0.5) * LOG2E
+    rows = out_ref.shape[0]
+    top = functools.reduce(jnp.maximum, [stat[0, 0] for stat in stats])
+    weights = [stat[0, 1] * jnp.exp2((stat[0, 0] - top) * factor) for stat in stats]
     whole = functools.reduce(jnp.add, weights)
-    rows, width = query.shape
-    total = 0.0
-    for (out, _), weight in zip(parts, weights):
-        share = (weight / whole).reshape(width // HD, rows).T
-        total = total + out.astype(jnp.float32).reshape(rows, width // HD, HD) * share[:, :, None]
-    return total.reshape(rows, width).astype(jnp.bfloat16)
+    shares = [weight / whole for weight in weights]
+    for head in range(group):
+        span = slice(head * HD, (head + 1) * HD)
+        terms = [
+            out[:, span].astype(jnp.float32)
+            * jnp.transpose(jnp.broadcast_to(share[head : head + 1, :], (HD, rows)))
+            for out, share in zip(outs, shares)
+        ]
+        out_ref[:, span] = functools.reduce(jnp.add, terms).astype(out_ref.dtype)
+
+
+def merge(parts, kv_heads):
+    count = len(parts)
+    rows, width = parts[0][0].shape
+    group = width // HD // kv_heads
+    wide = pl.BlockSpec((rows, group * HD), lambda g: (0, g))
+    return pl.pallas_call(
+        functools.partial(merge_kernel, count, group),
+        grid=(kv_heads,),
+        in_specs=[pl.BlockSpec((1, 2, group, rows), lambda g: (g, 0, 0, 0))] * count + [wide] * count,
+        out_specs=wide,
+        out_shape=jax.ShapeDtypeStruct((rows, width), jnp.bfloat16),
+        name="merge",
+    )(*[stat for _, stat in parts], *[out for out, _ in parts])
+
+
+def peers_of(me_a, me_b, n, m):
+    peers = [{"ba": lax.rem(me_b + k, m)} for k in range(1, m)]
+    peers += [{"aa": lax.rem(me_a + hop, n)} for hop in range(2, n, 2)]
+    return peers + [{"aa": partner_of(me_a)}]
+
+
+def partner_of(me_a):
+    return me_a + 1 - 2 * lax.rem(me_a, 2)
+
+
+def meet(peers):
+    barrier = pltpu.get_barrier_semaphore()
+    for peer in peers:
+        pl.semaphore_signal(barrier, inc=1, device_id=peer, device_id_type=pl.DeviceIdType.MESH)
+    pl.semaphore_wait(barrier, len(peers))
+
+
+def remote(source, target, send, receive, peer):
+    copy = pltpu.make_async_remote_copy(
+        src_ref=source,
+        dst_ref=target,
+        send_sem=send,
+        recv_sem=receive,
+        device_id=peer,
+        device_id_type=pl.DeviceIdType.MESH,
+    )
+    copy.start()
+    return copy
+
+
+def dispatch_kernel(n, m, packed, out, own_sem, z_send, z_recv, x_send, x_recv, c_send, c_recv):
+    me_a, me_b = lax.axis_index("aa"), lax.axis_index("ba")
+    slots, columns = packed.shape[1], packed.shape[2]
+    meet(peers_of(me_a, me_b, n, m))
+
+    def place(b, a):
+        if len(out.shape) == 3:
+            return out.at[a, pl.ds(pl.multiple_of(b * slots, slots), slots)]
+        return out.at[
+            pl.ds(pl.multiple_of(b * slots, slots), slots),
+            pl.ds(pl.multiple_of(a * columns, columns), columns),
+        ]
+
+    own = pltpu.make_async_copy(packed.at[me_b], place(me_b, me_a), own_sem)
+    own.start()
+    over_z = [None]
+    for k in range(1, m):
+        to = lax.rem(me_b + k, m)
+        over_z.append(
+            remote(packed.at[to], place(me_b, me_a), z_send.at[k], z_recv.at[k], {"ba": to})
+        )
+    partner = partner_of(me_a)
+    over_x, over_c = {}, {}
+
+    def forward(k):
+        b = lax.rem(me_b - k + m, m)
+        for j, hop in enumerate(range(2, n, 2), 1):
+            over_x[k, j].wait_recv()
+            block = place(b, lax.rem(me_a - hop + n, n))
+            over_c[k, j] = remote(
+                block, block, c_send.at[k, j], c_recv.at[k, j], {"aa": partner}
+            )
+
+    for k in range(m):
+        if k == 0:
+            own.wait()
+        else:
+            over_z[k].wait_recv()
+        block = place(lax.rem(me_b - k + m, m), me_a)
+        for j, hop in enumerate(range(2, n, 2), 1):
+            over_x[k, j] = remote(
+                block,
+                block,
+                x_send.at[k, j],
+                x_recv.at[k, j],
+                {"aa": lax.rem(me_a + hop, n)},
+            )
+        over_c[k, 0] = remote(block, block, c_send.at[k, 0], c_recv.at[k, 0], {"aa": partner})
+        if k > 0:
+            forward(k - 1)
+    forward(m - 1)
+    for copy in over_c.values():
+        copy.wait_recv()
+    for copy in over_z[1:] + list(over_x.values()) + list(over_c.values()):
+        copy.wait_send()
+
+
+def dispatch(packed):
+    n, m = lax.axis_size("aa"), lax.axis_size("ba")
+    columns = packed.shape[1]
+    rows = packed.shape[0] // m
+    half = n // 2
+    sems = [pltpu.SemaphoreType.DMA((m,))] * 2 + [pltpu.SemaphoreType.DMA((m, half))] * 4
+    flat = columns % LANES == 0
+    shape = (m * rows, n * columns) if flat else (n, m * rows, columns)
+    out = pl.pallas_call(
+        functools.partial(dispatch_kernel, n, m),
+        out_shape=jax.ShapeDtypeStruct(shape, packed.dtype),
+        in_specs=[pl.BlockSpec(memory_space=pltpu.VMEM)],
+        out_specs=pl.BlockSpec(memory_space=pltpu.VMEM),
+        scratch_shapes=[pltpu.SemaphoreType.DMA] + sems,
+        compiler_params=pltpu.CompilerParams(
+            collective_id=1, has_side_effects=True, vmem_limit_bytes=24 * 1024 * 1024
+        ),
+        name="dispatch",
+    )(packed.reshape(m, rows, columns))
+    return out if flat else out.transpose(1, 0, 2).reshape(m * rows, n * columns)
+
+
+def combine_kernel(
+    n, m, part, out, near, summed, far, total, own_sem, z_send, z_recv, x_send, x_recv, c_send, c_recv
+):
+    me_a, me_b = lax.axis_index("aa"), lax.axis_index("ba")
+    slots, columns = out.shape[1], out.shape[2]
+    meet(peers_of(me_a, me_b, n, m))
+    partner = partner_of(me_a)
+
+    def piece(k, a):
+        b = lax.rem(me_b + k, m)
+        if len(part.shape) == 3:
+            return part.at[a, pl.ds(pl.multiple_of(b * slots, slots), slots)]
+        return part.at[
+            pl.ds(pl.multiple_of(b * slots, slots), slots),
+            pl.ds(pl.multiple_of(a * columns, columns), columns),
+        ]
+
+    order = list(range(1, m)) + [0]
+    over_c, over_x = {}, {}
+    over_z = [None] * m
+    for k in order:
+        for j in range(n // 2):
+            over_c[k, j] = remote(
+                piece(k, lax.rem(partner + 2 * j, n)),
+                near.at[k, j],
+                c_send.at[k, j],
+                c_recv.at[k, j],
+                {"aa": partner},
+            )
+
+    def join(k, j):
+        over_c[k, j].wait_recv()
+        mine = piece(k, lax.rem(me_a + 2 * j, n))
+        return mine[...].astype(jnp.float32) + near[k, j].astype(jnp.float32)
+
+    def finish(k):
+        value = join(k, 0)
+        for j in range(1, n // 2):
+            over_x[k, j].wait_recv()
+            value = value + far[k, j].astype(jnp.float32)
+        total[k] = value.astype(total.dtype)
+        if k == 0:
+            copy = pltpu.make_async_copy(total.at[0], out.at[me_b], own_sem)
+            copy.start()
+            copy.wait()
+        else:
+            over_z[k] = remote(
+                total.at[k],
+                out.at[me_b],
+                z_send.at[k],
+                z_recv.at[k],
+                {"ba": lax.rem(me_b + k, m)},
+            )
+
+    for k in order:
+        for j in range(1, n // 2):
+            summed[k, j] = join(k, j).astype(summed.dtype)
+            over_x[k, j] = remote(
+                summed.at[k, j],
+                far.at[k, j],
+                x_send.at[k, j],
+                x_recv.at[k, j],
+                {"aa": lax.rem(me_a + 2 * j, n)},
+            )
+    for k in order:
+        finish(k)
+    for copy in over_z[1:]:
+        copy.wait_recv()
+    for copy in over_z[1:] + list(over_x.values()) + list(over_c.values()):
+        copy.wait_send()
+
+
+def combine(part):
+    n, m = lax.axis_size("aa"), lax.axis_size("ba")
+    rows, columns = part.shape[0] // m, part.shape[1] // n
+    if columns % LANES:
+        part = part.reshape(m * rows, n, columns).transpose(1, 0, 2)
+    half = n // 2
+    sems = [pltpu.SemaphoreType.DMA((m,))] * 2 + [pltpu.SemaphoreType.DMA((m, half))] * 4
+    block = pltpu.VMEM((m, half, rows, columns), part.dtype)
+    out = pl.pallas_call(
+        functools.partial(combine_kernel, n, m),
+        out_shape=jax.ShapeDtypeStruct((m, rows, columns), part.dtype),
+        in_specs=[pl.BlockSpec(memory_space=pltpu.VMEM)],
+        out_specs=pl.BlockSpec(memory_space=pltpu.VMEM),
+        scratch_shapes=[block, block, block, pltpu.VMEM((m, rows, columns), part.dtype)]
+        + [pltpu.SemaphoreType.DMA]
+        + sems,
+        compiler_params=pltpu.CompilerParams(
+            collective_id=2, has_side_effects=True, vmem_limit_bytes=40 * 1024 * 1024
+        ),
+        name="combine",
+    )(part)
+    return out.reshape(m * rows, columns)
 
 
 def on_device(
@@ -194,26 +422,17 @@
     packed = lax.dot_general(
         placing, expert_in, (((0,), (0,)), ((), ())), preferred_element_type=jnp.float32
     ).astype(jnp.bfloat16)
-    arrived = lax.all_to_all(packed, "ba", split_axis=0, concat_axis=0, tiled=True)
+    piece = dispatch(packed)
     gate_w = expert_gate[0]
     up_w = expert_up[0]
     down_w = expert_down[0]
-    piece = lax.all_gather(arrived, "aa", axis=1, tiled=True)
     gate_part = jnp.dot(piece, gate_w, preferred_element_type=jnp.float32)
     up_part = jnp.dot(piece, up_w, preferred_element_type=jnp.float32)
     act = (jax.nn.silu(gate_part) * up_part).astype(jnp.bfloat16)
-    expert_out = lax.psum_scatter(
-        lax.dot_general(
-            down_w, act, (((0,), (1,)), ((), ())), preferred_element_type=jnp.float32
-        ).astype(jnp.bfloat16),
-        "aa",
-        scatter_dimension=0,
-        tiled=True,
+    returned = combine(
+        jnp.dot(act, down_w, preferred_element_type=jnp.float32).astype(jnp.bfloat16)
     )
-    returned = lax.all_to_all(expert_out, "ba", split_axis=1, concat_axis=1, tiled=True)
-    from_experts = lax.dot_general(
-        placing, returned, (((1,), (1,)), ((), ())), preferred_element_type=jnp.float32
-    )
+    from_experts = jnp.dot(placing, returned, preferred_element_type=jnp.float32)
     return (hidden + gate[:, None] * from_experts).astype(jnp.bfloat16)
 
 

time: 413 us -> 330 us (0.80); the launches traced: 412 us -> 334 us
  waiting for transfers between devices: 222 us -> 100 us
  Pallas kernels: 49 us -> 140 us
  blocking collectives: 40.6 us -> 6.28 us
  local copies, waits for them, and re-layouts: 20.7 us -> 12.1 us
  other arithmetic: 6.67 us -> 2.26 us
    pallas_call x0 -> x3, Pallas kernels: none -> 92.6 us  [the longest x1 47.3 us: combine(): pl.pallas_call(functools.partial(combine_kernel, n, m), out_shape=jax.Sha...]
    reduce_scatter x1 -> x0, waiting for transfers between devices: 51.3 us -> none  [on_device(): lax.psum_scatter(lax.dot_general(down_w, act, (((0,), (1,)), ((), ())), p...]
    all_gather x1 -> x0, waiting for transfers between devices: 39.6 us -> none  [on_device(): piece = lax.all_gather(arrived, 'aa', axis=1, tiled=True)]
    all_to_all x1 -> x0, blocking collectives: 34.3 us -> none  [on_device(): lax.all_to_all(packed, 'ba', split_axis=0, concat_axis=0, tiled=True)]
    all_to_all x1 -> x0, waiting for transfers between devices: 31.3 us -> none  [on_device(): lax.all_to_all(expert_out, 'ba', split_axis=1, concat_axis=1, tiled=True)]
    ppermute x1, waiting for transfers between devices: 0.01 us -> 13.1 us  [span_attention(): far.append((lax.ppermute(query, 'aa', ahead), [(j, i) for i, j in ahead]))]
    mul x6 -> x0, local copies, waits for them, and re-layouts: 11.9 us -> none  [span_attention(): out.astype(jnp.float32).reshape(rows, width // HD, HD) * share[:, :, None]]
    all_gather x1, waiting for transfers between devices: 44.6 us -> 34.5 us  [on_device(): attended = lax.all_gather(own, 'aa', axis=0, tiled=True)]
  transfers between devices with their start and end apart: 11 -> 8, of which waited for: 6 -> 4; matrix products, arithmetic and copies ran while one was open for 3% -> 0% of each run, Pallas kernels for 6% -> 7%
where the time goes in v2:
time: 330 us; the launch traced here: 334 us
  Pallas kernels  140 us (42%)
  waiting for transfers between devices  100 us (30%)
  matrix products  40.4 us (12%)
  starting transfers between devices  18.1 us (5%)
  between operations  14.2 us (4%)
  local copies, waits for them, and re-layouts  12.1 us (4%)
  blocking collectives  6.28 us (2%)
    reduce_scatter x1, waiting for transfers between devices, on_device(): lax.psum_scatter(jnp.dot(attended, out_weight, preferred_element_type=jnp...  51.8 us
    pallas_call x3, Pallas kernels, attend(): pl.pallas_call(functools.partial(attend_kernel, shards, group), grid_spec...  47.6 us
    pallas_call x1, Pallas kernels, combine(): pl.pallas_call(functools.partial(combine_kernel, n, m), out_shape=jax.Sha...  47.3 us
    pallas_call x1, Pallas kernels, dispatch(): pl.pallas_call(functools.partial(dispatch_kernel, n, m), out_shape=jax.Sh...  41.8 us
    all_gather x1, waiting for transfers between devices, on_device(): attended = lax.all_gather(own, 'aa', axis=0, tiled=True)  34.5 us
    dot_general x1, matrix products, on_device(): jnp.dot(act, down_w, preferred_element_type=jnp.float32)  20.6 us
    ppermute x1, waiting for transfers between devices, span_attention(): far.append((lax.ppermute(query, 'aa', ahead), [(j, i) for i, j in ahead]))  13.1 us
    unnamed x44, local copies, waits for them, and re-layouts  12.1 us
  transfers between devices with their start and end apart: 8, of which 4 were waited for; matrix products, arithmetic and copies ran while one was open for 0% of the time, Pallas kernels for 7%

profile of v2, /device:TPU:0, one launch (start us, length us, event | category | flops | bytes accessed | tf_op | source)
XLA Modules:
  0.0 333.6 jit_solution(17473086720733537721)
XLA Ops:
  6.5 0.0 copy-start
  6.5 0.0 all-gather.2.cloned.1.call-start
  6.5 0.5 collective-permute-start.2
  7.0 0.0 collective-permute-start.3
  7.1 3.0 collective-permute-start.1
  10.0 0.0 collective-permute-start
  10.7 0.6 collective-permute-done.lengths
  11.3 0.7 pad_add_fusion.lengths
  12.0 13.1 %collective-permute-done.1.q_ref = bf16[256,1280]{1,0:T(8,128)(2,1)S(1)} collective-permute-done((bf16[256,1280]{1,0:T(8,128)(2,1)}, bf16[256,1280]{1,0:T(8,128)(2,1)S(1)}, u32[]{:S(2)}, u32[]{:S(2)}) %collective-permute-start.1) | collective-permute-done | bytes 655392 | tf_op jit(solution)/shard_map/ppermute | solution.py:124
  25.1 0.0 collective-permute-done.2.refs_1_.refs_0_
  25.1 0.0 collective-permute-done.3.refs_3_.refs_1_
  25.1 0.0 copy-start.8
  25.1 1.2 copy-done.8
  26.4 0.0 copy-start.10
  26.4 1.2 copy-done.10
  27.6 0.0 copy-start.9
  27.6 23.2 %attend.4 = (bf16[256,1280]{1,0:T(8,128)(2,1)S(1)}, f32[2,2,5,256]{3,2,1,0:T(8,128)S(1)}) custom-call(s32[2]{0:T(128)S(1)} %pad_add_fusion.lengths, bf16[256,1280]{1,0:T(8,128)(2,1)S(1)} %collective-permute-done.1.q_ref, bf16[2048,256]{1,0:T(8,128)(2,1)S(1)} %copy-done.8, bf16[2048,256]{1,0:T(8,128)(2,1)S(1)} %collective-permute-done.2.refs_1_.refs_0_, ...), custom_call_target="tpu_custom_call" | custom-call | flops 10737418240 | bytes 6160384 | tf_op jit(solution)/shard_map/attend/pallas_call | solution.py:88
  50.8 10.3 %collective-permute-start.5 = (bf16[256,1280]{1,0:T(8,128)(2,1)S(1)}, bf16[256,1280]{1,0:T(8,128)(2,1)S(1)}, u32[]{:S(2)}, u32[]{:S(2)}) collective-permute-start(bf16[256,1280]{1,0:T(8,128)(2,1)S(1)} %get-tuple-element.15), channel_id=1, source_target_pairs={{8,0},{12,4},{0,8},{4,12},{9,1},{13,5},{1,9},{5,13},{10,2},{14,6},... | collective-permute-start | bytes 1966088 | tf_op jit(solution)/shard_map/ppermute | solution.py:132
  61.1 0.0 copy-done.9
  61.1 0.0 copy-done.11
  61.1 9.6 %attend.3 = (f32[256,1280]{1,0:T(8,128)S(1)}, f32[2,2,5,256]{3,2,1,0:T(8,128)S(1)}) custom-call(s32[1]{0:T(128)S(6)} %copy.14.lengths, bf16[256,1280]{1,0:T(8,128)(2,1)S(1)} %copy-done.11, bf16[2048,256]{1,0:T(8,128)(2,1)S(1)} %copy-done.9, bf16[2048,256]{1,0:T(8,128)(2,1)S(1)} %copy-done.10), custom_call_target="tpu_custom_call" | custom-call | flops 5368709120 | bytes 4063232 | tf_op jit(solution)/shard_map/attend/pallas_call | solution.py:88
  70.8 0.0 copy-start.4
  70.8 1.1 copy-done.4
  71.8 0.6 copy-done.6
  72.5 4.3 %collective-permute-start.4 = (f32[2,2,5,256]{3,2,1,0:T(8,128)S(1)}, f32[2,2,5,256]{3,2,1,0:T(8,128)S(1)}, u32[]{:S(2)}, u32[]{:S(2)}) collective-permute-start(f32[2,2,5,256]{3,2,1,0:T(8,128)S(1)} %get-tuple-element.12), channel_id=1, source_target_pairs={{8,0},{12,4},{0,8},{4,12},{9,1},{13,5},{1,9},{5,13},{10,2},{14,6},... | collective-permute-start | bytes 61448 | tf_op jit(solution)/shard_map/ppermute | solution.py:132
  76.8 14.7 %attend.5 = (f32[256,1280]{1,0:T(8,128)S(1)}, f32[2,2,5,256]{3,2,1,0:T(8,128)S(1)}) custom-call(s32[1]{0:T(128)} %collective-permute-done.lengths, bf16[256,1280]{1,0:T(8,128)(2,1)S(1)} %copy-done.11, bf16[2048,256]{1,0:T(8,128)(2,1)S(1)} %collective-permute-done.2.refs_1_.refs_0_, bf16[2048,256]{1,0:T(8,128)(2,1)S(1)} %collective-permute-done.3.refs_3_.refs_1_), custom_call_target="tpu_custom_call" | custom-call | flops 5368709120 | bytes 4063232 | tf_op jit(solution)/shard_map/attend/pallas_call | solution.py:88
  91.5 0.0 copy-start.5
  91.5 1.0 copy-done.5
  92.6 0.6 copy-done.7
  93.2 0.0 collective-permute-done.4.refs_1_
  93.2 0.0 collective-permute-done.5.refs_4_
  93.2 0.0 copy-start.16
  93.2 0.8 copy-done.16
  94.0 0.0 copy-done.17
  94.0 3.5 %merge.1 = bf16[256,1280]{1,0:T(8,128)(2,1)} custom-call(f32[2,2,5,256]{3,2,1,0:T(8,128)} %copy-done.6, f32[2,2,5,256]{3,2,1,0:T(8,128)} %copy-done.17, f32[2,2,5,256]{3,2,1,0:T(8,128)} %copy-done.7, f32[256,1280]{1,0:T(8,128)} %copy-done.4, bf16[256,1280]{1,0:T(8,128)(2,1)} %copy-done.16, f32[256,1280]{1,0:T(8,128)} %copy-done.5), custom_call_target="tpu_custom_call" | custom-call | tf_op jit(solution)/shard_map/merge/pallas_call | solution.py:160
  97.5 0.0 all-gather.2.cloned.1.call-update
  97.5 0.0 reduce-scatter.2.cloned.1.call-start
  97.5 34.5 %all-gather.2.cloned.1.call-done = bf16[1024,1280]{1,0:T(8,128)(2,1)} async-done(((bf16[256,1280]{1,0:T(8,128)(2,1)}), bf16[1024,1280]{1,0:T(8,128)(2,1)}) %all-gather.2.cloned.1.call-update) | async-done | bytes 2621456 | tf_op jit(solution)/shard_map/all_gather | solution.py:391
  132.0 0.0 copy-done
  132.0 6.9 %convolution_convert_fusion = bf16[1024,1280]{1,0:T(8,128)(2,1)} fusion(bf16[1024,1280]{1,0:T(8,128)(2,1)} %all-gather.2.cloned.1.call-done, bf16[1280,1280]{1,0:T(8,128)(2,1)S(1)} %copy-done), kind=kOutput, calls=%fused_computation.7 | convolution fusion | flops 3356753920 | bytes 8519680 | tf_op jit(solution)/shard_map/dot_general | solution.py:393
  138.9 0.0 copy-start.19
  138.9 0.0 reduce-scatter.2.cloned.1.call-update
  138.9 0.6 copy-done.21
  139.5 0.0 copy-done.20
  139.6 51.8 %reduce-scatter.2.cloned.1.call-done = bf16[256,1280]{1,0:T(8,128)(2,1)} async-done(((bf16[1024,1280]{1,0:T(8,128)(2,1)}), bf16[256,1280]{1,0:T(8,128)(2,1)}) %reduce-scatter.2.cloned.1.call-update) | async-done | bytes 655376 | tf_op jit(solution)/shard_map/reduce_scatter | solution.py:392
  191.3 0.0 copy-done.12
  191.3 1.4 multiply_reduce_fusion
  192.8 0.0 copy-done.18
  192.8 0.0 copy-done.19
  192.8 2.3 fusion.15
  195.1 6.3 %psum.7 = f32[256,5]{0,1:T(8,128)S(1)} all-reduce(f32[256,5]{0,1:T(8,128)S(1)} %pad_maximum_fusion), channel_id=1, replica_groups=mesh['ga'=2,'aa'=4,'ba'=4] {'aa'}, use_global_device_ids=true, to_apply=%region_2.0 | all-reduce | flops 1280 | bytes 10240 | tf_op jit(solution)/shard_map/psum | solution.py:399
  201.4 0.0 copy-done.14
  201.5 0.8 convolution_convert_fusion.1
  202.2 41.8 %dispatch.1 = bf16[512,5120]{1,0:T(8,128)(2,1)S(1)} custom-call(bf16[4,128,1280]{2,1,0:T(8,128)(2,1)S(1)} %bitcast.26), custom_call_target="tpu_custom_call" | custom-call | tf_op jit(solution)/shard_map/dispatch/pallas_call | solution.py:265
  244.1 0.0 copy-start.2
  244.1 2.3 copy-done.2
  246.4 8.5 %fusion.2 = f32[512,1024]{1,0:T(8,128)S(1)} fusion(bf16[512,5120]{1,0:T(8,128)(2,1)S(1)} %dispatch.1, bf16[1,5120,1024]{2,1,0:T(8,128)(2,1)} %param.24), kind=kOutput, calls=%fused_computation.2 | convolution fusion | flops 5368709120 | bytes 17825792 | tf_op jit(solution)/shard_map/dot_general | solution.py:430
  254.9 20.6 %fusion.6.part = bf16[512,5120]{1,0:T(8,128)(2,1)} fusion(bf16[1,1024,5120]{2,1,0:T(8,128)(2,1)} %param.25, f32[512,1024]{1,0:T(8,128)S(1)} %fusion.2, bf16[512,5120]{1,0:T(8,128)(2,1)} %copy-done.2, bf16[1,5120,1024]{2,1,0:T(8,128)(2,1)} %param.23), kind=kOutput, calls=%fused_computation.6 | convolution fusion | flops 10743185408 | bytes 33554432 | tf_op jit(solution)/shard_map/dot_general | solution.py:433
  275.5 2.5 copy-done.3
  278.0 47.3 %combine.1 = bf16[4,128,1280]{2,1,0:T(8,128)(2,1)S(1)} custom-call(bf16[512,5120]{1,0:T(8,128)(2,1)S(1)} %copy-done.3), custom_call_target="tpu_custom_call" | custom-call | tf_op jit(solution)/shard_map/combine/pallas_call | solution.py:359
  325.3 0.0 copy-done.13
  325.3 0.0 copy-done.15
  325.3 1.4 fusion.10
  326.7 0.0 copy-done.1
  (18 shorter events, 0.1 us)
Async XLA Ops:
  6.5 125.5 %copy-start = (bf16[1280,1280]{1,0:T(8,128)(2,1)S(1)}, bf16[1280,1280]{1,0:T(8,128)(2,1)}, u32[]{:S(2)}) copy-start(bf16[1280,1280]{1,0:T(8,128)(2,1)} %param.18) | copy-start | bytes 9830404
  6.5 125.5 %all-gather.2.cloned.1.call-start = ((), (), s32[]{:S(2)}) async-start(), calls=%async_computation.1 | async-start | bytes 3276800 | tf_op jit(solution)/shard_map/all_gather | solution.py:391
  6.5 18.6 %collective-permute-start.2 = (bf16[2048,256]{1,0:T(8,128)(2,1)}, bf16[2048,256]{1,0:T(8,128)(2,1)S(1)}, u32[]{:S(2)}, u32[]{:S(2)}) collective-permute-start(bf16[2048,256]{1,0:T(8,128)(2,1)} %refs_0_.3), channel_id=1, source_target_pairs={{0,4},{4,0},{8,12},{12,8},{1,5},{5,1},{9,13},{13,9},{2,6},{6,2},{1... | collective-permute-start | bytes 3145736 | tf_op jit(solution)/shard_map/ppermute | solution.py:125
  7.0 18.1 %collective-permute-start.3 = (bf16[2048,256]{1,0:T(8,128)(2,1)}, bf16[2048,256]{1,0:T(8,128)(2,1)S(1)}, u32[]{:S(2)}, u32[]{:S(2)}) collective-permute-start(bf16[2048,256]{1,0:T(8,128)(2,1)} %refs_2_.1), channel_id=1, source_target_pairs={{0,4},{4,0},{8,12},{12,8},{1,5},{5,1},{9,13},{13,9},{2,6},{6,2},{1... | collective-permute-start | bytes 3145736 | tf_op jit(solution)/shard_map/ppermute | solution.py:126
  7.1 18.1 %collective-permute-start.1 = (bf16[256,1280]{1,0:T(8,128)(2,1)}, bf16[256,1280]{1,0:T(8,128)(2,1)S(1)}, u32[]{:S(2)}, u32[]{:S(2)}) collective-permute-start(bf16[256,1280]{1,0:T(8,128)(2,1)} %q_ref.3), channel_id=1, source_target_pairs={{0,8},{4,12},{8,0},{12,4},{1,9},{5,13},{9,1},{13,5},{2,10},{6,14},... | collective-permute-start | bytes 1966088 | tf_op jit(solution)/shard_map/ppermute | solution.py:124
  10.0 1.3 collective-permute-start
  25.1 1.2 copy-start.8
  26.4 1.2 copy-start.10
  27.6 33.6 %copy-start.9 = (bf16[2048,256]{1,0:T(8,128)(2,1)S(1)}, bf16[2048,256]{1,0:T(8,128)(2,1)}, u32[]{:S(2)}) copy-start(bf16[2048,256]{1,0:T(8,128)(2,1)} %refs_0_.3) | copy-start | bytes 3145732
  27.6 33.6 %copy-start.11 = (bf16[256,1280]{1,0:T(8,128)(2,1)S(1)}, bf16[256,1280]{1,0:T(8,128)(2,1)}, u32[]{:S(2)}) copy-start(bf16[256,1280]{1,0:T(8,128)(2,1)} %q_ref.3) | copy-start | bytes 1966084
  50.8 42.3 %collective-permute-start.5 = (bf16[256,1280]{1,0:T(8,128)(2,1)S(1)}, bf16[256,1280]{1,0:T(8,128)(2,1)S(1)}, u32[]{:S(2)}, u32[]{:S(2)}) collective-permute-start(bf16[256,1280]{1,0:T(8,128)(2,1)S(1)} %get-tuple-element.15), channel_id=1, source_target_pairs={{8,0},{12,4},{0,8},{4,12},{9,1},{13,5},{1,9},{5,13},{10,2},{14,6},... | collective-permute-start | bytes 1966088 | tf_op jit(solution)/shard_map/ppermute | solution.py:132
  70.8 1.1 copy-start.4
  71.8 0.6 copy-start.6
  72.5 20.7 %collective-permute-start.4 = (f32[2,2,5,256]{3,2,1,0:T(8,128)S(1)}, f32[2,2,5,256]{3,2,1,0:T(8,128)S(1)}, u32[]{:S(2)}, u32[]{:S(2)}) collective-permute-start(f32[2,2,5,256]{3,2,1,0:T(8,128)S(1)} %get-tuple-element.12), channel_id=1, source_target_pairs={{8,0},{12,4},{0,8},{4,12},{9,1},{13,5},{1,9},{5,13},{10,2},{14,6},... | collective-permute-start | bytes 61448 | tf_op jit(solution)/shard_map/ppermute | solution.py:132
  91.5 1.1 copy-start.5
  92.6 0.6 copy-start.7
  93.2 0.8 copy-start.17
  93.2 0.8 copy-start.16
  97.5 93.8 %reduce-scatter.2.cloned.1.call-start = ((), (), s32[]{:S(2)}) async-start(), calls=%async_computation.2 | async-start | bytes 3276800 | tf_op jit(solution)/shard_map/reduce_scatter | solution.py:392
  138.9 0.7 copy-start.21
  138.9 0.7 copy-start.20
  138.9 52.5 %copy-start.12 = (bf16[256,1280]{1,0:T(8,128)(2,1)S(1)}, bf16[256,1280]{1,0:T(8,128)(2,1)}, u32[]{:S(2)}) copy-start(bf16[256,1280]{1,0:T(8,128)(2,1)} %param.17) | copy-start | bytes 1966084
  138.9 53.9 %copy-start.18 = (f32[1280,4]{0,1:T(4,128)S(1)}, f32[1280,4]{0,1:T(4,128)}, u32[]{:S(2)}) copy-start(f32[1280,4]{0,1:T(4,128)} %param.20) | copy-start | bytes 61444
  138.9 53.9 %copy-start.19 = (f32[1280]{0:T(1024)S(1)}, f32[1280]{0:T(1024)}, u32[]{:S(2)}) copy-start(f32[1280]{0:T(1024)} %param.19) | copy-start | bytes 15364
  191.3 10.1 %copy-start.14 = (bf16[256,1280]{1,0:T(8,128)(2,1)S(1)}, bf16[256,1280]{1,0:T(8,128)(2,1)}, u32[]{:S(2)}) copy-start(bf16[256,1280]{1,0:T(8,128)(2,1)} %reduce-scatter.2.cloned.1.call-done) | copy-start | bytes 1966084
  244.1 2.3 copy-start.2
  275.5 2.5 copy-start.3
  278.0 47.3 %copy-start.13 = (bf16[256,1280]{1,0:T(8,128)(2,1)S(1)}, bf16[256,1280]{1,0:T(8,128)(2,1)}, u32[]{:S(2)}) copy-start(bf16[256,1280]{1,0:T(8,128)(2,1)} %param.17) | copy-start | bytes 1966084
  278.0 47.3 %copy-start.15 = (bf16[256,1280]{1,0:T(8,128)(2,1)S(1)}, bf16[256,1280]{1,0:T(8,128)(2,1)}, u32[]{:S(2)}) copy-start(bf16[256,1280]{1,0:T(8,128)(2,1)} %reduce-scatter.2.cloned.1.call-done) | copy-start | bytes 1966084
  278.0 48.7 %copy-start.1 = (bf16[1280,1280]{1,0:T(8,128)(2,1)S(1)}, bf16[1280,1280]{1,0:T(8,128)(2,1)}, u32[]{:S(2)}) copy-start(bf16[1280,1280]{1,0:T(8,128)(2,1)} %param.18) | copy-start | bytes 9830404
Sparse Core Ops, SparseCore 0:
  97.6 34.3 all-gather.1
  139.0 52.2 reduce-scatter.1

commit v3 on v2

--- a/solution.py
+++ b/solution.py
@@ -128,6 +128,7 @@
     both = jnp.concatenate([cache_lengths, near_length])
     parts = [attend(query, [keys], [values], cache_lengths, jnp.float32)]
     for rows, back in far:
+        rows, parts[0] = lax.optimization_barrier((rows, parts[0]))
         out, stat = attend(rows, [keys, near_keys], [values, near_values], both, jnp.bfloat16)
         parts.append((lax.ppermute(out, "aa", back), lax.ppermute(stat, "aa", back)))
     parts.append(attend(query, [near_keys], [near_values], near_length, jnp.float32))
@@ -197,10 +198,13 @@
     return copy
 
 
-def dispatch_kernel(n, m, packed, out, own_sem, z_send, z_recv, x_send, x_recv, c_send, c_recv):
+def dispatch_kernel(local, n, m, packed, out, own_sem, z_send, z_recv, x_send, x_recv, c_send, c_recv):
     me_a, me_b = lax.axis_index("aa"), lax.axis_index("ba")
     slots, columns = packed.shape[1], packed.shape[2]
-    meet(peers_of(me_a, me_b, n, m))
+    meet(peers_of(me_a, me_b, n, 1 if local else m))
+
+    def index(k):
+        return k if local else lax.rem(me_b - k + m, m)
 
     def place(b, a):
         if len(out.shape) == 3:
@@ -210,10 +214,12 @@
             pl.ds(pl.multiple_of(a * columns, columns), columns),
         ]
 
-    own = pltpu.make_async_copy(packed.at[me_b], place(me_b, me_a), own_sem)
-    own.start()
+    own = []
+    for k in range(m if local else 1):
+        own.append(pltpu.make_async_copy(packed.at[index(k)], place(index(k), me_a), own_sem.at[k]))
+        own[k].start()
     over_z = [None]
-    for k in range(1, m):
+    for k in range(1, 1 if local else m):
         to = lax.rem(me_b + k, m)
         over_z.append(
             remote(packed.at[to], place(me_b, me_a), z_send.at[k], z_recv.at[k], {"ba": to})
@@ -222,7 +228,7 @@
     over_x, over_c = {}, {}
 
     def forward(k):
-        b = lax.rem(me_b - k + m, m)
+        b = index(k)
         for j, hop in enumerate(range(2, n, 2), 1):
             over_x[k, j].wait_recv()
             block = place(b, lax.rem(me_a - hop + n, n))
@@ -231,11 +237,11 @@
             )
 
     for k in range(m):
-        if k == 0:
-            own.wait()
+        if k < len(own):
+            own[k].wait()
         else:
             over_z[k].wait_recv()
-        block = place(lax.rem(me_b - k + m, m), me_a)
+        block = place(index(k), me_a)
         for j, hop in enumerate(range(2, n, 2), 1):
             over_x[k, j] = remote(
                 block,
@@ -254,25 +260,27 @@
         copy.wait_send()
 
 
-def dispatch(packed):
-    n, m = lax.axis_size("aa"), lax.axis_size("ba")
+def dispatch(packed, local, m, name, number):
+    n = lax.axis_size("aa")
     columns = packed.shape[1]
     rows = packed.shape[0] // m
     half = n // 2
     sems = [pltpu.SemaphoreType.DMA((m,))] * 2 + [pltpu.SemaphoreType.DMA((m, half))] * 4
-    flat = columns % LANES == 0
+    flat = columns % LANES == 0 and not local
     shape = (m * rows, n * columns) if flat else (n, m * rows, columns)
     out = pl.pallas_call(
-        functools.partial(dispatch_kernel, n, m),
+        functools.partial(dispatch_kernel, local, n, m),
         out_shape=jax.ShapeDtypeStruct(shape, packed.dtype),
         in_specs=[pl.BlockSpec(memory_space=pltpu.VMEM)],
         out_specs=pl.BlockSpec(memory_space=pltpu.VMEM),
-        scratch_shapes=[pltpu.SemaphoreType.DMA] + sems,
+        scratch_shapes=[pltpu.SemaphoreType.DMA((m,))] + sems,
         compiler_params=pltpu.CompilerParams(
-            collective_id=1, has_side_effects=True, vmem_limit_bytes=24 * 1024 * 1024
-        ),
-        name="dispatch",
+            collective_id=number, has_side_effects=True, vmem_limit_bytes=24 * 1024 * 1024
+        ),
+        name=name,
     )(packed.reshape(m, rows, columns))
+    if local:
+        return out.reshape(n * m * rows, columns)
     return out if flat else out.transpose(1, 0, 2).reshape(m * rows, n * columns)
 
 
@@ -388,7 +396,7 @@
     expert_down,
 ):
     own = span_attention(query, keys, values, cache_lengths)
-    attended = lax.all_gather(own, "aa", axis=0, tiled=True)
+    attended = dispatch(own, True, 4 if own.shape[0] % 64 == 0 else 1, "gather", 3)
     hidden = residual.astype(jnp.float32) + lax.psum_scatter(
         jnp.dot(attended, out_weight, preferred_element_type=jnp.float32).astype(jnp.bfloat16),
         "ba",
@@ -422,7 +430,7 @@
     packed = lax.dot_general(
         placing, expert_in, (((0,), (0,)), ((), ())), preferred_element_type=jnp.float32
     ).astype(jnp.bfloat16)
-    piece = dispatch(packed)
+    piece = dispatch(packed, False, lax.axis_size("ba"), "dispatch", 1)
     gate_w = expert_gate[0]
     up_w = expert_up[0]
     down_w = expert_down[0]

time: 330 us -> 317 us (0.961); the launches traced: 334 us -> 317 us
  waiting for transfers between devices: 100 us -> 55.7 us
  Pallas kernels: 140 us -> 173 us
  starting transfers between devices: 18.1 us -> 12.4 us
    all_gather x1 -> x0, waiting for transfers between devices: 34.5 us -> none  [on_device(): attended = lax.all_gather(own, 'aa', axis=0, tiled=True)]
    pallas_call x1 -> x2, Pallas kernels: 41.8 us -> 66.3 us  [dispatch(): pl.pallas_call(functools.partial(dispatch_kernel, local, n, m), out_shape...]
    ppermute x1, waiting for transfers between devices: 13.1 us -> 0.01 us  [span_attention(): far.append((lax.ppermute(query, 'aa', ahead), [(j, i) for i, j in ahead]))]
    pallas_call x3, Pallas kernels: 47.6 us -> 56.1 us  [attend(): pl.pallas_call(functools.partial(attend_kernel, shards, group), grid_spec...]
    ppermute x1, starting transfers between devices: 4.3 us -> 0.08 us  [span_attention(): lax.ppermute(stat, 'aa', back)]
    ppermute x1, waiting for transfers between devices: 0.01 us -> 3.6 us  [span_attention(): lax.ppermute(stat, 'aa', back)]
    unnamed x44 -> x48, local copies, waits for them, and re-layouts: 12.1 us -> 14.3 us
  transfers between devices with their start and end apart: 8 -> 7, of which waited for: 4 -> 2; matrix products, arithmetic and copies ran while one was open for 0% -> 0% of each run, Pallas kernels for 7% -> 9%
where the time goes in v3:
time: 317 us
  Pallas kernels  173 us (55%)
  waiting for transfers between devices  55.7 us (18%)
  matrix products  38.4 us (12%)
  local copies, waits for them, and re-layouts  14.3 us (5%)
  between operations  14.3 us (5%)
  starting transfers between devices  12.4 us (4%)
  blocking collectives  6.28 us (2%)
    pallas_call x2, Pallas kernels, dispatch(): pl.pallas_call(functools.partial(dispatch_kernel, local, n, m), out_shape...  66.3 us
    pallas_call x3, Pallas kernels, attend(): pl.pallas_call(functools.partial(attend_kernel, shards, group), grid_spec...  56.1 us
    reduce_scatter x1, waiting for transfers between devices, on_device(): lax.psum_scatter(jnp.dot(attended, out_weight, preferred_element_type=jnp...  52 us
    pallas_call x1, Pallas kernels, combine(): pl.pallas_call(functools.partial(combine_kernel, n, m), out_shape=jax.Sha...  47.3 us
    dot_general x1, matrix products, on_device(): jnp.dot(act, down_w, preferred_element_type=jnp.float32)  20.6 us
    unnamed x48, local copies, waits for them, and re-layouts  14.3 us
    ppermute x1, starting transfers between devices, span_attention(): lax.ppermute(out, 'aa', back)  8.87 us
    dot_general x1, matrix products, on_device(): up_part = jnp.dot(piece, up_w, preferred_element_type=jnp.float32)  8.47 us
  transfers between devices with their start and end apart: 7, of which 2 were waited for; matrix products, arithmetic and copies ran while one was open for 0% of the time, Pallas kernels for 9%

profile of v3, /device:TPU:0, one launch (start us, length us, event | category | flops | bytes accessed | tf_op | source)
XLA Modules:
  0.0 316.8 jit_solution(7194386437834805218)
XLA Ops:
  6.5 0.0 copy-start
  6.5 0.0 reduce-scatter.2.cloned.1.call-start
  6.5 0.5 collective-permute-start.2
  7.0 0.0 collective-permute-start.3
  7.1 3.0 collective-permute-start
  10.0 0.0 collective-permute-start.1
  10.7 0.0 copy-start.9
  10.7 1.2 copy-done.9
  11.9 0.0 copy-start.11
  11.9 1.2 copy-done.11
  13.1 0.0 copy-start.13
  13.1 1.1 copy-done.13
  14.2 0.0 copy-start.10
  14.2 18.1 %attend.3 = (f32[256,1280]{1,0:T(8,128)S(1)}, f32[2,2,5,256]{3,2,1,0:T(8,128)S(1)}) custom-call(s32[1]{0:T(128)S(6)} %copy.14.lengths, bf16[256,1280]{1,0:T(8,128)(2,1)S(1)} %copy-done.13, bf16[2048,256]{1,0:T(8,128)(2,1)S(1)} %copy-done.9, bf16[2048,256]{1,0:T(8,128)(2,1)S(1)} %copy-done.11), custom_call_target="tpu_custom_call" | custom-call | flops 5368709120 | bytes 4063232 | tf_op jit(solution)/shard_map/attend/pallas_call | solution.py:88
  32.3 0.0 copy-start.5
  32.4 1.1 copy-done.5
  33.4 0.6 copy-done.7
  34.0 0.0 collective-permute-done.1.lengths
  34.0 0.7 pad_add_fusion.lengths
  34.8 0.0 collective-permute-done.q_ref
  34.8 0.0 collective-permute-done.2.refs_1_.refs_0_
  34.8 0.0 collective-permute-done.3.refs_3_.refs_1_
  34.8 0.0 copy-done.10
  34.8 0.0 copy-done.12
  34.8 27.5 %attend.4 = (bf16[256,1280]{1,0:T(8,128)(2,1)S(1)}, f32[2,2,5,256]{3,2,1,0:T(8,128)S(1)}) custom-call(s32[2]{0:T(128)S(1)} %pad_add_fusion.lengths, bf16[256,1280]{1,0:T(8,128)(2,1)S(1)} %collective-permute-done.q_ref, bf16[2048,256]{1,0:T(8,128)(2,1)S(1)} %copy-done.10, bf16[2048,256]{1,0:T(8,128)(2,1)S(1)} %collective-permute-done.2.refs_1_.refs_0_, ...), custom_call_target="tpu_custom_call" | custom-call | flops 10737418240 | bytes 6160384 | tf_op jit(solution)/shard_map/attend/pallas_call | solution.py:88
  62.3 8.9 %collective-permute-start.5 = (bf16[256,1280]{1,0:T(8,128)(2,1)S(1)}, bf16[256,1280]{1,0:T(8,128)(2,1)S(1)}, u32[]{:S(2)}, u32[]{:S(2)}) collective-permute-start(bf16[256,1280]{1,0:T(8,128)(2,1)S(1)} %get-tuple-element.21), channel_id=1, source_target_pairs={{8,0},{12,4},{0,8},{4,12},{9,1},{13,5},{1,9},{5,13},{10,2},{14,6},... | collective-permute-start | bytes 1966088 | tf_op jit(solution)/shard_map/ppermute | solution.py:133
  71.2 0.1 collective-permute-start.4
  71.3 10.5 %attend.5 = (f32[256,1280]{1,0:T(8,128)S(1)}, f32[2,2,5,256]{3,2,1,0:T(8,128)S(1)}) custom-call(s32[1]{0:T(128)} %collective-permute-done.1.lengths, bf16[256,1280]{1,0:T(8,128)(2,1)S(1)} %copy-done.13, bf16[2048,256]{1,0:T(8,128)(2,1)S(1)} %collective-permute-done.2.refs_1_.refs_0_, bf16[2048,256]{1,0:T(8,128)(2,1)S(1)} %collective-permute-done.3.refs_3_.refs_1_), custom_call_target="tpu_custom_call" | custom-call | flops 5368709120 | bytes 4063232 | tf_op jit(solution)/shard_map/attend/pallas_call | solution.py:88
  81.8 0.0 copy-start.6
  81.8 1.1 copy-done.6
  82.8 0.6 copy-done.8
  83.4 3.6 %collective-permute-done.4.refs_1_ = f32[2,2,5,256]{3,2,1,0:T(8,128)S(1)} collective-permute-done((f32[2,2,5,256]{3,2,1,0:T(8,128)S(1)}, f32[2,2,5,256]{3,2,1,0:T(8,128)S(1)}, u32[]{:S(2)}, u32[]{:S(2)}) %collective-permute-start.4) | collective-permute-done | bytes 20512 | tf_op jit(solution)/shard_map/ppermute | solution.py:133
  87.0 0.0 collective-permute-done.5.refs_4_
  87.1 0.8 copy-done.18
  87.9 0.0 copy-done.19
  87.9 3.4 %merge.1 = bf16[256,1280]{1,0:T(8,128)(2,1)} custom-call(f32[2,2,5,256]{3,2,1,0:T(8,128)} %copy-done.7, f32[2,2,5,256]{3,2,1,0:T(8,128)} %copy-done.19, f32[2,2,5,256]{3,2,1,0:T(8,128)} %copy-done.8, f32[256,1280]{1,0:T(8,128)} %copy-done.5, bf16[256,1280]{1,0:T(8,128)(2,1)} %copy-done.18, f32[256,1280]{1,0:T(8,128)} %copy-done.6), custom_call_target="tpu_custom_call" | custom-call | tf_op jit(solution)/shard_map/merge/pallas_call | solution.py:161
  91.3 1.1 copy-done.4
  92.4 24.5 %gather.1 = bf16[4,256,1280]{2,1,0:T(8,128)(2,1)S(1)} custom-call(bf16[4,64,1280]{2,1,0:T(8,128)(2,1)S(1)} %bitcast.28), custom_call_target="tpu_custom_call" | custom-call | tf_op jit(solution)/shard_map/gather/pallas_call | solution.py:271
  116.9 0.0 copy-done
  116.9 4.8 %convolution_convert_fusion = bf16[1024,1280]{1,0:T(8,128)(2,1)} fusion(bf16[1024,1280]{1,0:T(8,128)(2,1)S(1)} %bitcast.27, bf16[1280,1280]{1,0:T(8,128)(2,1)S(1)} %copy-done), kind=kOutput, calls=%fused_computation.7 | convolution fusion | flops 3356753920 | bytes 8519680 | tf_op jit(solution)/shard_map/dot_general | solution.py:401
  121.8 0.0 copy-start.21
  121.8 0.0 reduce-scatter.2.cloned.1.call-update
  121.8 0.6 copy-done.23
  122.5 0.0 copy-done.22
  122.5 52.0 %reduce-scatter.2.cloned.1.call-done = bf16[256,1280]{1,0:T(8,128)(2,1)} async-done(((bf16[1024,1280]{1,0:T(8,128)(2,1)}), bf16[256,1280]{1,0:T(8,128)(2,1)}) %reduce-scatter.2.cloned.1.call-update) | async-done | bytes 655376 | tf_op jit(solution)/shard_map/reduce_scatter | solution.py:400
  174.5 0.0 copy-done.14
  174.5 1.4 multiply_reduce_fusion
  176.0 0.0 copy-done.20
  176.0 0.0 copy-done.21
  176.0 2.3 fusion.15
  178.3 6.3 %psum.7 = f32[256,5]{0,1:T(8,128)S(1)} all-reduce(f32[256,5]{0,1:T(8,128)S(1)} %pad_maximum_fusion), channel_id=1, replica_groups=mesh['ga'=2,'aa'=4,'ba'=4] {'aa'}, use_global_device_ids=true, to_apply=%region_2.0 | all-reduce | flops 1280 | bytes 10240 | tf_op jit(solution)/shard_map/psum | solution.py:407
  184.6 0.0 copy-done.16
  184.6 0.8 convolution_convert_fusion.1
  185.4 41.8 %dispatch.1 = bf16[512,5120]{1,0:T(8,128)(2,1)S(1)} custom-call(bf16[4,128,1280]{2,1,0:T(8,128)(2,1)S(1)} %bitcast.30), custom_call_target="tpu_custom_call" | custom-call | tf_op jit(solution)/shard_map/dispatch/pallas_call | solution.py:271
  227.2 0.0 copy-start.2
  227.2 2.3 copy-done.2
  229.6 8.5 %fusion.2 = f32[512,1024]{1,0:T(8,128)S(1)} fusion(bf16[512,5120]{1,0:T(8,128)(2,1)S(1)} %dispatch.1, bf16[1,5120,1024]{2,1,0:T(8,128)(2,1)} %param.24), kind=kOutput, calls=%fused_computation.2 | convolution fusion | flops 5368709120 | bytes 17825792 | tf_op jit(solution)/shard_map/dot_general | solution.py:438
  238.0 20.6 %fusion.6.part = bf16[512,5120]{1,0:T(8,128)(2,1)} fusion(bf16[1,1024,5120]{2,1,0:T(8,128)(2,1)} %param.25, f32[512,1024]{1,0:T(8,128)S(1)} %fusion.2, bf16[512,5120]{1,0:T(8,128)(2,1)} %copy-done.2, bf16[1,5120,1024]{2,1,0:T(8,128)(2,1)} %param.23), kind=kOutput, calls=%fused_computation.6 | convolution fusion | flops 10743185408 | bytes 33554432 | tf_op jit(solution)/shard_map/dot_general | solution.py:441
  258.7 2.5 copy-done.3
  261.2 47.3 %combine.1 = bf16[4,128,1280]{2,1,0:T(8,128)(2,1)S(1)} custom-call(bf16[512,5120]{1,0:T(8,128)(2,1)S(1)} %copy-done.3), custom_call_target="tpu_custom_call" | custom-call | tf_op jit(solution)/shard_map/combine/pallas_call | solution.py:367
  308.5 0.0 copy-done.15
  308.5 0.0 copy-done.17
  308.5 1.4 fusion.10
  309.9 0.0 copy-done.1
  (20 shorter events, 0.1 us)
Async XLA Ops:
  6.5 110.4 %copy-start = (bf16[1280,1280]{1,0:T(8,128)(2,1)S(1)}, bf16[1280,1280]{1,0:T(8,128)(2,1)}, u32[]{:S(2)}) copy-start(bf16[1280,1280]{1,0:T(8,128)(2,1)} %param.18) | copy-start | bytes 9830404
  6.5 168.0 %reduce-scatter.2.cloned.1.call-start = ((), (), s32[]{:S(2)}) async-start(), calls=%async_computation.1 | async-start | bytes 3276800 | tf_op jit(solution)/shard_map/reduce_scatter | solution.py:400
  6.5 28.3 %collective-permute-start.2 = (bf16[2048,256]{1,0:T(8,128)(2,1)}, bf16[2048,256]{1,0:T(8,128)(2,1)S(1)}, u32[]{:S(2)}, u32[]{:S(2)}) collective-permute-start(bf16[2048,256]{1,0:T(8,128)(2,1)} %refs_0_.3), channel_id=1, source_target_pairs={{0,4},{4,0},{8,12},{12,8},{1,5},{5,1},{9,13},{13,9},{2,6},{6,2},{1... | collective-permute-start | bytes 3145736 | tf_op jit(solution)/shard_map/ppermute | solution.py:125
  7.0 27.8 %collective-permute-start.3 = (bf16[2048,256]{1,0:T(8,128)(2,1)}, bf16[2048,256]{1,0:T(8,128)(2,1)S(1)}, u32[]{:S(2)}, u32[]{:S(2)}) collective-permute-start(bf16[2048,256]{1,0:T(8,128)(2,1)} %refs_2_.1), channel_id=1, source_target_pairs={{0,4},{4,0},{8,12},{12,8},{1,5},{5,1},{9,13},{13,9},{2,6},{6,2},{1... | collective-permute-start | bytes 3145736 | tf_op jit(solution)/shard_map/ppermute | solution.py:126
  7.1 27.7 %collective-permute-start = (bf16[256,1280]{1,0:T(8,128)(2,1)}, bf16[256,1280]{1,0:T(8,128)(2,1)S(1)}, u32[]{:S(2)}, u32[]{:S(2)}) collective-permute-start(bf16[256,1280]{1,0:T(8,128)(2,1)} %q_ref.3), channel_id=1, source_target_pairs={{0,8},{4,12},{8,0},{12,4},{1,9},{5,13},{9,1},{13,5},{2,10},{6,14},... | collective-permute-start | bytes 1966088 | tf_op jit(solution)/shard_map/ppermute | solution.py:124
  10.0 24.0 %collective-permute-start.1 = (s32[1]{0:T(128)}, s32[1]{0:T(128)}, u32[]{:S(2)}, u32[]{:S(2)}) collective-permute-start(s32[1]{0:T(128)} %param.16), channel_id=1, source_target_pairs={{0,4},{4,0},{8,12},{12,8},{1,5},{5,1},{9,13},{13,9},{2,6},{6,2},{1... | collective-permute-start | bytes 20 | tf_op jit(solution)/shard_map/ppermute | solution.py:127
  10.7 1.2 copy-start.9
  11.9 1.2 copy-start.11
  13.1 1.1 copy-start.13
  14.2 20.6 %copy-start.10 = (bf16[2048,256]{1,0:T(8,128)(2,1)S(1)}, bf16[2048,256]{1,0:T(8,128)(2,1)}, u32[]{:S(2)}) copy-start(bf16[2048,256]{1,0:T(8,128)(2,1)} %refs_0_.3) | copy-start | bytes 3145732
  14.2 20.6 %copy-start.12 = (bf16[2048,256]{1,0:T(8,128)(2,1)S(1)}, bf16[2048,256]{1,0:T(8,128)(2,1)}, u32[]{:S(2)}) copy-start(bf16[2048,256]{1,0:T(8,128)(2,1)} %refs_2_.1) | copy-start | bytes 3145732
  32.3 1.1 copy-start.5
  33.4 0.6 copy-start.7
  62.3 24.7 %collective-permute-start.5 = (bf16[256,1280]{1,0:T(8,128)(2,1)S(1)}, bf16[256,1280]{1,0:T(8,128)(2,1)S(1)}, u32[]{:S(2)}, u32[]{:S(2)}) collective-permute-start(bf16[256,1280]{1,0:T(8,128)(2,1)S(1)} %get-tuple-element.21), channel_id=1, source_target_pairs={{8,0},{12,4},{0,8},{4,12},{9,1},{13,5},{1,9},{5,13},{10,2},{14,6},... | collective-permute-start | bytes 1966088 | tf_op jit(solution)/shard_map/ppermute | solution.py:133
  71.2 15.9 %collective-permute-start.4 = (f32[2,2,5,256]{3,2,1,0:T(8,128)S(1)}, f32[2,2,5,256]{3,2,1,0:T(8,128)S(1)}, u32[]{:S(2)}, u32[]{:S(2)}) collective-permute-start(f32[2,2,5,256]{3,2,1,0:T(8,128)S(1)} %get-tuple-element.18), channel_id=1, source_target_pairs={{8,0},{12,4},{0,8},{4,12},{9,1},{13,5},{1,9},{5,13},{10,2},{14,6},... | collective-permute-start | bytes 61448 | tf_op jit(solution)/shard_map/ppermute | solution.py:133
  81.8 1.1 copy-start.6
  82.8 0.6 copy-start.8
  87.0 0.8 copy-start.19
  87.0 0.8 copy-start.18
  91.3 1.1 copy-start.4
  121.8 0.7 copy-start.23
  121.8 0.7 copy-start.22
  121.8 52.7 %copy-start.14 = (bf16[256,1280]{1,0:T(8,128)(2,1)S(1)}, bf16[256,1280]{1,0:T(8,128)(2,1)}, u32[]{:S(2)}) copy-start(bf16[256,1280]{1,0:T(8,128)(2,1)} %param.17) | copy-start | bytes 1966084
  121.8 54.2 %copy-start.20 = (f32[1280,4]{0,1:T(4,128)S(1)}, f32[1280,4]{0,1:T(4,128)}, u32[]{:S(2)}) copy-start(f32[1280,4]{0,1:T(4,128)} %param.20) | copy-start | bytes 61444
  121.8 54.2 %copy-start.21 = (f32[1280]{0:T(1024)S(1)}, f32[1280]{0:T(1024)}, u32[]{:S(2)}) copy-start(f32[1280]{0:T(1024)} %param.19) | copy-start | bytes 15364
  174.5 10.1 %copy-start.16 = (bf16[256,1280]{1,0:T(8,128)(2,1)S(1)}, bf16[256,1280]{1,0:T(8,128)(2,1)}, u32[]{:S(2)}) copy-start(bf16[256,1280]{1,0:T(8,128)(2,1)} %reduce-scatter.2.cloned.1.call-done) | copy-start | bytes 1966084
  227.2 2.4 copy-start.2
  258.7 2.5 copy-start.3
  261.2 47.3 %copy-start.15 = (bf16[256,1280]{1,0:T(8,128)(2,1)S(1)}, bf16[256,1280]{1,0:T(8,128)(2,1)}, u32[]{:S(2)}) copy-start(bf16[256,1280]{1,0:T(8,128)(2,1)} %param.17) | copy-start | bytes 1966084
  261.2 47.4 %copy-start.17 = (bf16[256,1280]{1,0:T(8,128)(2,1)S(1)}, bf16[256,1280]{1,0:T(8,128)(2,1)}, u32[]{:S(2)}) copy-start(bf16[256,1280]{1,0:T(8,128)(2,1)} %reduce-scatter.2.cloned.1.call-done) | copy-start | bytes 1966084
  261.2 48.8 %copy-start.1 = (bf16[1280,1280]{1,0:T(8,128)(2,1)S(1)}, bf16[1280,1280]{1,0:T(8,128)(2,1)}, u32[]{:S(2)}) copy-start(bf16[1280,1280]{1,0:T(8,128)(2,1)} %param.18) | copy-start | bytes 9830404
Sparse Core Ops, SparseCore 0:
  121.9 52.5 reduce-scatter.1
